TPU v7x, 128 devices: a whole 4x4x4 slice. The times are simulated.
128 devices in a mesh: seq: 16 (over z, x), head: 8 (over y, core).
Axes of the slice: x: 4, y: 4, z: 4, core: 2. Of those that a mesh axis runs over, the one named last changes fastest.
Arguments:
- hidden_in: bfloat16 [65536, 1024], P('seq'), may hold values from -6 to 6
- norm_gain: bfloat16 [1024], replicated, may hold values from 0.099609375 to 1.8984375
- gate_weight: bfloat16 [1024, 2048], P(None, 'head'), may hold values from -0.1875 to 0.1875
- value_weight: bfloat16 [1024, 2048], P(None, 'head'), may hold values from -0.375 to 0.375
- state_weight: bfloat16 [1024, 256], replicated, may hold values from -0.1875 to 0.1875
- step_weight: bfloat16 [1024, 32], P(None, 'head'), may hold values from -0.1875 to 0.1875
- step_bias: float32 [32], P('head'), may hold values from -1 to 1
- decay_log: float32 [32], P('head'), may hold values from -16 to -3
- skip_gain: float32 [32], P('head'), may hold values from 0.5 to 1.5
- conv_value: bfloat16 [4, 2048], P(None, 'head'), may hold values from -3 to 3
- conv_state: bfloat16 [4, 256], replicated, may hold values from -3 to 3
- output_gain: bfloat16 [2048], P('head'), may hold values from 0.099609375 to 1.8984375
- output_weight: bfloat16 [2048, 1024], P('head'), may hold values from -0.125 to 0.125
- piece_lengths: int32 [16], replicated, may hold values from 1 to 32768, 65536 in all
Outputs:
- block_out: bfloat16 [65536, 1024], P(('seq', 'head'))
Inputs may be any that keep to these rules, and one draw needn't show every extreme that they name: `piece_lengths`: the lengths sum to 65536; the pieces lie end to end from position 0.
All inputs are finite; a program needn't handle non-finite values.
Results may differ from a plain program's by a relative error of at most 0.018.
Values may be sent and summed in bfloat16 or wider, within the bound.
A program may use at most 128 MiB of HBM per device.

v0:
```python
import functools
import math

import jax
import jax.numpy as jnp
from jax import lax
from jax.experimental import pallas as pl
from jax.experimental.pallas import tpu as pltpu
from jax.sharding import PartitionSpec as P

HEAD_DIM = 64
STATE = 128
CONV = 4
CHUNK = 128
PIECES = 16
HALO = 8
RESET = 256.0
LOG2E = math.log2(math.e)

f32 = jnp.float32
bf16 = jnp.bfloat16
epsilon = 1e-05
MESH = pl.DeviceIdType.MESH
NN = (((1,), (0,)), ((), ()))
NT = (((1,), (1,)), ((), ()))
TN = (((0,), (0,)), ((), ()))


def mm(a, b, dims=NN, precision=None):
    return lax.dot_general(a, b, dims, precision=precision, preferred_element_type=f32)


def silu(x):
    half = 0.5 * x
    return half * jnp.tanh(half) + half


def normalized(h, gain):
    wide = h.astype(f32)
    scale = lax.rsqrt(jnp.mean(wide * wide, axis=1, keepdims=True) + epsilon)
    return (wide * scale * gain.astype(f32)).astype(bf16)


def whole(shape):
    zeros = (0,) * len(shape)
    return pl.BlockSpec(shape, lambda *_: zeros)


SMEM_SPEC = pl.BlockSpec(memory_space=pltpu.SMEM)
ANY_SPEC = pl.BlockSpec(memory_space=pl.ANY)


def params(**kw):
    return pltpu.CompilerParams(vmem_limit_bytes=60 * 1024 * 1024, **kw)


def project_kernel(h_ref, gain_ref, gw_ref, vw_ref, sw_ref, tw_ref, gate_ref, mix_ref, raw_ref):
    inner = vw_ref.shape[1]
    n = normalized(h_ref[...], gain_ref[...])
    gate_ref[...] = mm(n, gw_ref[...]).astype(bf16)
    mix_ref[:, :inner] = mm(n, vw_ref[...]).astype(bf16)
    mix_ref[:, inner:] = mm(n, sw_ref[...]).astype(bf16)
    raw = mm(tw_ref[...], n, NT)
    for q in range(raw.shape[1] // CHUNK):
        raw_ref[q] = raw[:, q * CHUNK : (q + 1) * CHUNK]


def project(hidden, gain, gw, vw, sw, tw):
    tokens, width = hidden.shape
    inner = vw.shape[1]
    mixed = inner + sw.shape[1]
    rows = 512
    return pl.pallas_call(
        project_kernel,
        grid=(tokens // rows,),
        in_specs=[
            pl.BlockSpec((rows, width), lambda i: (i, 0)),
            whole(gain.shape),
            whole(gw.shape),
            whole(vw.shape),
            whole(sw.shape),
            whole(tw.shape),
        ],
        out_specs=[
            pl.BlockSpec((rows, inner), lambda i: (i, 0)),
            pl.BlockSpec((rows, mixed), lambda i: (i, 0)),
            pl.BlockSpec((rows // CHUNK, 8, CHUNK), lambda i: (i, 0, 0)),
        ],
        out_shape=[
            jax.ShapeDtypeStruct((tokens, inner), bf16),
            jax.ShapeDtypeStruct((tokens, mixed), bf16),
            jax.ShapeDtypeStruct((tokens // CHUNK, 8, CHUNK), f32),
        ],
        compiler_params=params(),
        cost_estimate=pl.CostEstimate(
            flops=2 * tokens * width * 1024, bytes_accessed=20 << 20, transcendentals=0
        ),
        name="project",
    )(hidden, gain, gw, vw, sw, tw)


def head_lanes(columns):
    low = lax.broadcasted_iota(jnp.int32, (columns[0].shape[0], 2 * HEAD_DIM), 1) < HEAD_DIM
    pairs = [
        jnp.where(low, columns[2 * p], columns[2 * p + 1]) for p in range(len(columns) // 2)
    ]
    return jnp.concatenate(pairs, axis=1)


def decays(first_row, raw, lens_ref, bias_ref, rate_ref):
    chunks = raw.shape[0]
    shape = (chunks, 8, CHUNK)
    sub = lax.broadcasted_iota(jnp.int32, shape, 1)
    upper = sub < 4
    head = jnp.where(upper, sub, sub - 4)
    pos = (
        first_row
        + lax.broadcasted_iota(jnp.int32, shape, 0) * CHUNK
        + lax.broadcasted_iota(jnp.int32, shape, 2)
    )
    start = jnp.zeros(shape, jnp.int32)
    stop = jnp.full(shape, 1 << 30, jnp.int32)
    edge = jnp.int32(0)
    for k in range(PIECES):
        start = jnp.where(pos >= edge, edge, start)
        edge = edge + lens_ref[k]
        stop = jnp.minimum(stop, jnp.where(edge > pos, edge, 1 << 30))
    since = pos - start
    until = stop - 1 - pos
    bias = jnp.zeros(shape, f32)
    rate = jnp.zeros(shape, f32)
    for h in range(4):
        bias = jnp.where(head == h, bias_ref[h], bias)
        rate = jnp.where(head == h, rate_ref[h], rate)
    rate = jnp.exp(rate) * (-LOG2E)
    z = raw + bias
    step = jnp.maximum(z, 0.0) + jnp.log1p(jnp.exp(-jnp.abs(z)))
    log = step * rate
    reset = jnp.where(since == 0, -RESET, 0.0)
    ones = (
        lax.broadcasted_iota(jnp.int32, (CHUNK, CHUNK), 0)
        <= lax.broadcasted_iota(jnp.int32, (CHUNK, CHUNK), 1)
    ).astype(f32)
    cum = mm(
        (log + reset).reshape(chunks * 8, CHUNK), ones, precision=lax.Precision.HIGHEST
    ).reshape(shape)
    excl = cum - log
    total = cum[:, :, CHUNK - 1 :]
    log_step = jnp.log2(step)
    row = jnp.where(upper, cum - log_step, excl + log_step)
    g1 = jnp.where(upper, cum, excl)
    g2 = jnp.where(upper, jnp.exp2(cum), jnp.exp2(total - cum) * step)
    g3 = jnp.where(upper, jnp.exp2(total - excl), jnp.exp2(excl) * step)
    g4 = jnp.where(upper, since, until).astype(f32)
    return row, g1, g2, g3, g4


def states_kernel(
    axis,
    mix_ref,
    before_ref,
    after_ref,
    halo_ref,
    gain_ref,
    vw_ref,
    sw_ref,
    raw_ref,
    lens_ref,
    bias_ref,
    rate_ref,
    cv_ref,
    cs_ref,
    conv_ref,
    fresh_ref,
    cols_ref,
    row_ref,
    end_ref,
    total_ref,
    ext,
    halo,
    run,
    reach,
):
    c = pl.program_id(0)
    count = pl.num_programs(0)
    inner = vw_ref.shape[1]
    mixed = mix_ref.shape[1]

    @pl.when(c == 0)
    def _():
        n = normalized(halo_ref[...], gain_ref[...])
        halo[:, :inner] = mm(n, vw_ref[...]).astype(bf16).astype(f32)
        halo[:, inner:] = mm(n, sw_ref[...]).astype(bf16).astype(f32)
        first_row = lax.axis_index(axis) * (count * CHUNK)
        row, g1, g2, g3, g4 = decays(first_row, raw_ref[...], lens_ref, bias_ref, rate_ref)
        row_ref[...] = row
        cols_ref[:, 0:8, :] = g1
        cols_ref[:, 8:16, :] = g2
        cols_ref[:, 16:24, :] = g3
        cols_ref[:, 24:32, :] = g4
        run[...] = jnp.zeros_like(run)
        reach[...] = jnp.zeros_like(reach)

    ext[HALO : HALO + CHUNK, :] = mix_ref[...].astype(f32)

    @pl.when(c == 0)
    def _():
        ext[0:HALO, :] = halo[0:HALO, :]

    @pl.when(c > 0)
    def _():
        ext[0:HALO, :] = before_ref[...].astype(f32)[HALO:, :]

    @pl.when(c == count - 1)
    def _():
        ext[HALO + CHUNK :, :] = halo[HALO:, :]

    @pl.when(c < count - 1)
    def _():
        ext[HALO + CHUNK :, :] = after_ref[...].astype(f32)[:HALO, :]

    cols = cols_ref[c]
    turned = jnp.concatenate([cols, jnp.zeros((CHUNK - 32, CHUNK), f32)], axis=0).T
    width = 128
    since = jnp.broadcast_to(turned[:, 24:25], (CHUNK, width))
    until = jnp.broadcast_to(turned[:, 28:29], (CHUNK, width))
    taps = jnp.concatenate([cv_ref[...], cs_ref[...]], axis=1).astype(f32)
    for reverse in (False, True):
        left = until if reverse else since
        for block in range(mixed // width):
            lanes = slice(block * width, (block + 1) * width)
            total = ext[HALO : HALO + CHUNK, lanes] * taps[CONV - 1 : CONV, lanes]
            for distance in range(1, CONV):
                at = HALO + distance if reverse else HALO - distance
                term = ext[at : at + CHUNK, lanes] * taps[CONV - 1 - distance : CONV - distance, lanes]
                total = total + jnp.where(left >= distance, term, 0.0)
            base = mixed if reverse else 0
            conv_ref[:, base + block * width : base + (block + 1) * width] = silu(total).astype(bf16)

    tails = (
        head_lanes([turned[:, 12 + h : 13 + h] for h in range(4)]),
        head_lanes([turned[:, 20 + h : 21 + h] for h in range(4)]),
    )
    passing = head_lanes([cols[h : h + 1, CHUNK - 1 :] for h in range(4)])
    for d in range(2):
        x = conv_ref[:, d * mixed : d * mixed + inner].astype(f32)
        write = conv_ref[:, d * mixed + inner : d * mixed + inner + STATE]
        scaled = (x * tails[d]).astype(bf16)
        fresh = mm(write, scaled, TN)
        fresh_ref[0, d] = fresh.astype(bf16)
        if d == 0:
            run[0] = run[0] * jnp.exp2(passing) + fresh
        else:
            run[1] = run[1] + jnp.exp2(reach[0:1, :]) * fresh
    reach[...] = reach[...] + passing

    @pl.when(c == count - 1)
    def _():
        end_ref[...] = run[...].astype(bf16)
        total_ref[...] = reach[...]


def states(axis, mix, halo, gain, vw, sw, raw, lens, bias, rate, cv, cs):
    tokens, mixed = mix.shape
    chunks = tokens // CHUNK
    inner = vw.shape[1]
    per = CHUNK // 16
    last = tokens // 16 - 1
    return pl.pallas_call(
        functools.partial(states_kernel, axis),
        grid=(chunks,),
        in_specs=[
            pl.BlockSpec((CHUNK, mixed), lambda c: (c, 0)),
            pl.BlockSpec((16, mixed), lambda c: (jnp.maximum(c * per - 1, 0), 0)),
            pl.BlockSpec((16, mixed), lambda c: (jnp.minimum(c * per + per, last), 0)),
            whole(halo.shape),
            whole(gain.shape),
            whole(vw.shape),
            whole(sw.shape),
            whole(raw.shape),
            SMEM_SPEC,
            SMEM_SPEC,
            SMEM_SPEC,
            whole(cv.shape),
            whole(cs.shape),
        ],
        out_specs=[
            pl.BlockSpec((CHUNK, 2 * mixed), lambda c: (c, 0)),
            pl.BlockSpec((1, 2, STATE, inner), lambda c: (c, 0, 0, 0)),
            whole((chunks, 32, CHUNK)),
            whole((chunks, 8, CHUNK)),
            whole((2, STATE, inner)),
            whole((8, inner)),
        ],
        out_shape=[
            jax.ShapeDtypeStruct((tokens, 2 * mixed), bf16),
            jax.ShapeDtypeStruct((chunks, 2, STATE, inner), bf16),
            jax.ShapeDtypeStruct((chunks, 32, CHUNK), f32),
            jax.ShapeDtypeStruct((chunks, 8, CHUNK), f32),
            jax.ShapeDtypeStruct((2, STATE, inner), bf16),
            jax.ShapeDtypeStruct((8, inner), f32),
        ],
        scratch_shapes=[
            pltpu.VMEM((CHUNK + 2 * HALO, mixed), f32),
            pltpu.VMEM((2 * HALO, mixed), f32),
            pltpu.VMEM((2, STATE, inner), f32),
            pltpu.VMEM((8, inner), f32),
        ],
        compiler_params=params(),
        name="states",
    )(mix, mix, mix, halo, gain, vw, sw, raw, lens, bias, rate, cv, cs)


def remote(src, dst, send, recv, **where):
    return pltpu.make_async_remote_copy(
        src_ref=src,
        dst_ref=dst,
        send_sem=send,
        recv_sem=recv,
        device_id=where,
        device_id_type=MESH,
    )


def greet(axes_and_peers):
    barrier = pltpu.get_barrier_semaphore()
    for where in axes_and_peers:
        pl.semaphore_signal(barrier, inc=1, device_id=where, device_id_type=MESH)
    pl.semaphore_wait(barrier, len(axes_and_peers))


def head_peer(me, chips, dy, dc):
    y, core = me // 2, me % 2
    return ((y + dy) % chips) * 2 + (core + dc) % 2


def exchange_kernel(
    seq_count,
    head_count,
    end_ref,
    total_ref,
    w_ref,
    in_ref,
    all_ref,
    ends,
    totals,
    end_send,
    end_recv,
    total_send,
    total_recv,
    w_send,
    w_recv,
):
    me = lax.axis_index("seq")
    head = lax.axis_index("head")
    chips = head_count // 2
    half = w_ref.shape[0] // 2
    up = head_peer(head, chips, 1, 0)
    down = head_peer(head, chips, chips - 1, 0)
    partner = head_peer(head, chips, 0, 1)
    greet(
        [{"seq": (me + k) % seq_count} for k in range(1, seq_count)]
        + [{"head": up}, {"head": down}, {"head": partner}]
    )
    started = []

    def start(copy):
        copy.start()
        started.append(copy)
        return copy

    near = start(remote(w_ref, all_ref.at[2], w_send.at[0], w_recv.at[0], head=up))
    far = start(remote(w_ref, all_ref.at[6], w_send.at[1], w_recv.at[1], head=down))
    beside = start(remote(w_ref, all_ref.at[1], w_send.at[2], w_recv.at[2], head=partner))
    for k in range(1, seq_count):
        target = (me + k) % seq_count
        backward = (me + k) // seq_count
        start(remote(end_ref.at[backward], ends.at[k], end_send.at[k], end_recv.at[k], seq=target))
        start(remote(total_ref, totals.at[k], total_send.at[k], total_recv.at[k], seq=target))

    near.wait_recv()
    top, bottom = pl.ds(0, half), pl.ds(half, half)
    t1 = start(remote(all_ref.at[2, top], all_ref.at[4, top], w_send.at[3], w_recv.at[3], head=up))
    t2 = start(remote(all_ref.at[2], all_ref.at[3], w_send.at[4], w_recv.at[4], head=partner))
    far.wait_recv()
    t3 = start(
        remote(all_ref.at[6, bottom], all_ref.at[4, bottom], w_send.at[5], w_recv.at[5], head=down)
    )
    t4 = start(remote(all_ref.at[6], all_ref.at[7], w_send.at[6], w_recv.at[6], head=partner))

    for k in range(1, seq_count):
        target = (me + k) % seq_count
        remote(end_ref.at[0], ends.at[k], end_send.at[k], end_recv.at[k], seq=target).wait_recv()
        remote(total_ref, totals.at[k], total_send.at[k], total_recv.at[k], seq=target).wait_recv()
    in_ref[...] = jnp.zeros_like(in_ref)
    for k in range(seq_count - 1, 0, -1):

        @pl.when(k <= me)
        def _(k=k):
            in_ref[0] = in_ref[0] * jnp.exp2(totals[k, 0:1, :]) + ends[k].astype(f32)

    for k in range(1, seq_count):

        @pl.when(k > me)
        def _(k=k):
            in_ref[1] = in_ref[1] * jnp.exp2(totals[k, 0:1, :]) + ends[k].astype(f32)

    t1.wait_recv()
    t3.wait_recv()
    t5 = start(remote(all_ref.at[4], all_ref.at[5], w_send.at[7], w_recv.at[7], head=partner))
    for copy in (beside, t2, t4, t5):
        copy.wait_recv()
    for copy in started:
        copy.wait_send()


def exchange(mesh_shape, end, total, w):
    seq_count, head_count = mesh_shape
    return pl.pallas_call(
        functools.partial(exchange_kernel, seq_count, head_count),
        in_specs=[whole(end.shape), whole(total.shape), ANY_SPEC],
        out_specs=[whole(end.shape), ANY_SPEC],
        out_shape=[
            jax.ShapeDtypeStruct(end.shape, f32),
            jax.ShapeDtypeStruct((head_count,) + w.shape, bf16),
        ],
        scratch_shapes=[
            pltpu.VMEM((seq_count,) + end.shape[1:], bf16),
            pltpu.VMEM((seq_count,) + total.shape, f32),
            pltpu.SemaphoreType.DMA((seq_count,)),
            pltpu.SemaphoreType.DMA((seq_count,)),
            pltpu.SemaphoreType.DMA((seq_count,)),
            pltpu.SemaphoreType.DMA((seq_count,)),
            pltpu.SemaphoreType.DMA((8,)),
            pltpu.SemaphoreType.DMA((8,)),
        ],
        compiler_params=params(collective_id=0, has_side_effects=True),
        name="exchange",
    )(end, total, w)


def outputs_kernel(
    conv_ref, gate_ref, cols_ref, row_ref, fresh_ref, in_ref, skip_ref, gf_ref, gb_ref, ss_ref, entry
):
    g = pl.program_id(0)
    chunks = fresh_ref.shape[0]
    inner = gate_ref.shape[1]
    mixed = conv_ref.shape[1] // 2
    group = conv_ref.shape[0] // CHUNK

    @pl.when(g == 0)
    def _():
        def passing(c):
            return jnp.exp2(head_lanes([cols_ref[c, h : h + 1, CHUNK - 1 :] for h in range(4)]))

        def forward(c, state):
            entry[0, c] = state.astype(bf16)
            return state * passing(c) + fresh_ref[c, 0].astype(f32)

        def backward(i, state):
            c = chunks - 1 - i
            entry[1, c] = state.astype(bf16)
            return state * passing(c) + fresh_ref[c, 1].astype(f32)

        lax.fori_loop(0, chunks, forward, in_ref[0])
        lax.fori_loop(0, chunks, backward, in_ref[1])

    i = lax.broadcasted_iota(jnp.int32, (CHUNK, CHUNK), 0)
    j = lax.broadcasted_iota(jnp.int32, (CHUNK, CHUNK), 1)
    lower = i >= j
    upper = i <= j
    low = j < HEAD_DIM
    skip = head_lanes([jnp.full((1, 1), skip_ref[h], f32) for h in range(4)])
    sub = lax.broadcasted_iota(jnp.int32, (8, CHUNK), 0)
    ones = jnp.ones((8, inner), bf16)
    sums = jnp.zeros((8, CHUNK), f32)
    for q in range(group):
        c = g * group + q
        rows = slice(q * CHUNK, (q + 1) * CHUNK)
        cols = cols_ref[c]
        turned = jnp.concatenate([cols, jnp.zeros((CHUNK - 32, CHUNK), f32)], axis=0).T
        row = row_ref[c]
        pair = []
        for d, keep in ((0, lower), (1, upper)):
            base = d * mixed + inner
            write = conv_ref[rows, base : base + STATE]
            read = conv_ref[rows, base + STATE : base + 2 * STATE]
            pair.append(jnp.where(keep, mm(read, write, NT), 0.0))
        weights = ([], [])
        for h in range(4):
            arg = jnp.where(
                lower,
                turned[:, h : h + 1] - row[h : h + 1, :],
                row[4 + h : 5 + h, :] - turned[:, 4 + h : 5 + h],
            )
            table = jnp.exp2(arg)
            for d in range(2):
                weights[d].append((pair[d] * table).astype(bf16))
        gate = silu(gate_ref[rows, :].astype(f32))
        opening = (8, 16)
        for d, out_ref in ((0, gf_ref), (1, gb_ref)):
            x = conv_ref[rows, d * mixed : d * mixed + inner]
            read = conv_ref[rows, d * mixed + inner + STATE : (d + 1) * mixed]
            local = []
            for p in range(2):
                half = x[:, p * CHUNK : (p + 1) * CHUNK]
                zero = jnp.zeros_like(half)
                stacked = jnp.concatenate(
                    [jnp.where(low, half, zero), jnp.where(low, zero, half)], axis=0
                )
                both = jnp.concatenate(weights[d][2 * p : 2 * p + 2], axis=1)
                local.append(mm(both, stacked))
            carried = mm(read, entry[d, c])
            open_at = opening[d]
            scale = head_lanes([turned[:, open_at + h : open_at + h + 1] for h in range(4)])
            out = jnp.concatenate(local, axis=1) + carried * scale + skip * x.astype(f32)
            gated = out * gate
            out_ref[rows, :] = gated.astype(bf16)
            square = mm(ones, (gated * gated).astype(bf16), NT)
            sums = jnp.where(sub == 2 * q + d, square, sums)
    ss_ref[...] = sums


def outputs(conv, gate, cols, row, fresh, incoming, skip):
    tokens, inner = gate.shape
    chunks = tokens // CHUNK
    rows = 4 * CHUNK
    return pl.pallas_call(
        outputs_kernel,
        grid=(tokens // rows,),
        in_specs=[
            pl.BlockSpec((rows, conv.shape[1]), lambda g: (g, 0)),
            pl.BlockSpec((rows, inner), lambda g: (g, 0)),
            whole(cols.shape),
            whole(row.shape),
            whole(fresh.shape),
            whole(incoming.shape),
            SMEM_SPEC,
        ],
        out_specs=[
            pl.BlockSpec((rows, inner), lambda g: (g, 0)),
            pl.BlockSpec((rows, inner), lambda g: (g, 0)),
            pl.BlockSpec((8, CHUNK), lambda g: (g, 0)),
        ],
        out_shape=[
            jax.ShapeDtypeStruct((tokens, inner), bf16),
            jax.ShapeDtypeStruct((tokens, inner), bf16),
            jax.ShapeDtypeStruct((2 * chunks, CHUNK), f32),
        ],
        scratch_shapes=[pltpu.VMEM((2, chunks, STATE, inner), bf16)],
        compiler_params=params(),
        name="outputs",
    )(conv, gate, cols, row, fresh, incoming, skip)


def finish_kernel(
    head_count,
    gf_ref,
    gb_ref,
    ss_ref,
    gain_ref,
    hidden_ref,
    w_ref,
    all_ref,
    out_ref,
    sums,
    sending,
    arrived,
    total,
    rest,
    ss_send,
    ss_recv,
    send,
    recv,
    load,
):
    me = lax.axis_index("head")
    chips = head_count // 2
    inner = gain_ref.shape[1]
    rows = out_ref.shape[0]
    lines = ss_ref.shape[0] // head_count
    slots = [(dy, dc) for dy in range(chips) for dc in range(2)]
    peers = [head_peer(me, chips, dy, dc) for dy, dc in slots]
    residual = pltpu.make_async_copy(
        hidden_ref.at[pl.ds(pl.multiple_of(me * rows, rows), rows), :], rest, load
    )
    residual.start()
    greet([{"head": p} for p in peers[1:]])
    started = []
    for k in range(1, head_count):
        copy = remote(ss_ref, sums.at[k], ss_send.at[k], ss_recv.at[k], head=peers[k])
        copy.start()
        started.append(copy)
    for copy in started:
        copy.wait_recv()
    squares = ss_ref[...]
    for k in range(1, head_count):
        squares = squares + sums[k]
    total[...] = lax.rsqrt(squares * (1.0 / (inner * head_count)) + epsilon)
    gain = gain_ref[...].astype(f32)

    def combine(owner, slot):
        scale = total[pl.ds(pl.multiple_of(owner * lines, lines), lines), :]
        scale = jnp.concatenate([scale, jnp.zeros((CHUNK - lines, CHUNK), f32)], axis=0).T
        for q in range(rows // CHUNK):
            at = pl.ds(pl.multiple_of(owner * rows + q * CHUNK, CHUNK), CHUNK)
            both = gf_ref[at, :].astype(f32) * scale[:, 2 * q : 2 * q + 1]
            both = both + gb_ref[at, :].astype(f32) * scale[:, 2 * q + 1 : 2 * q + 2]
            sending[slot, q * CHUNK : (q + 1) * CHUNK, :] = (both * gain).astype(bf16)

    order = sorted(range(1, head_count), key=lambda k: -min(slots[k][0], chips - slots[k][0]))
    copies = []
    for k in order:
        combine(peers[k], k)
        copy = remote(sending.at[k], arrived.at[k], send.at[k], recv.at[k], head=peers[k])
        copy.start()
        copies.append(copy)
    combine(me, 0)
    residual.wait()
    step = 256

    def add(rows_in, weight, first):
        for b in range(out_ref.shape[1] // step):
            lanes = slice(b * step, (b + 1) * step)
            term = mm(rows_in, weight[:, lanes])
            if first:
                rest_wide[:, lanes] = rest[:, lanes].astype(f32) + term
            else:
                rest_wide[:, lanes] = rest_wide[:, lanes] + term

    def body(rest_wide_ref):
        nonlocal rest_wide
        rest_wide = rest_wide_ref
        add(sending[0], w_ref[...], True)
        for copy, k in reversed(list(zip(copies, order))):
            copy.wait_recv()
            add(arrived[k], all_ref[k], False)
        out_ref[...] = rest_wide_ref[...].astype(bf16)

    rest_wide = None
    pl.run_scoped(body, pltpu.VMEM(out_ref.shape, f32))
    for copy in started + copies:
        copy.wait_send()


def finish(head_count, gf, gb, ss, gain, hidden, w, w_all):
    tokens, inner = gf.shape
    rows = tokens // head_count
    width = hidden.shape[1]
    return pl.pallas_call(
        functools.partial(finish_kernel, head_count),
        in_specs=[
            whole(gf.shape),
            whole(gb.shape),
            whole(ss.shape),
            whole(gain.shape),
            ANY_SPEC,
            whole(w.shape),
            whole(w_all.shape),
        ],
        out_specs=whole((rows, width)),
        out_shape=jax.ShapeDtypeStruct((rows, width), bf16),
        scratch_shapes=[
            pltpu.VMEM((head_count,) + ss.shape, f32),
            pltpu.VMEM((head_count, rows, inner), bf16),
            pltpu.VMEM((head_count, rows, inner), bf16),
            pltpu.VMEM(ss.shape, f32),
            pltpu.VMEM((rows, width), bf16),
            pltpu.SemaphoreType.DMA((head_count,)),
            pltpu.SemaphoreType.DMA((head_count,)),
            pltpu.SemaphoreType.DMA((head_count,)),
            pltpu.SemaphoreType.DMA((head_count,)),
            pltpu.SemaphoreType.DMA,
        ],
        compiler_params=params(collective_id=1, has_side_effects=True),
        name="finish",
    )(gf, gb, ss, gain, hidden, w, w_all)


def local(
    hidden_in,
    norm_gain,
    gate_weight,
    value_weight,
    state_weight,
    step_weight,
    step_bias,
    decay_log,
    skip_gain,
    conv_value,
    conv_state,
    output_gain,
    output_weight,
    piece_lengths,
):
    seq_count, head_count = lax.axis_size("seq"), lax.axis_size("head")
    up = [(i, i + 1) for i in range(seq_count - 1)]
    down = [(j, i) for i, j in up]
    before = lax.ppermute(hidden_in[-HALO:], "seq", up)
    after = lax.ppermute(hidden_in[:HALO], "seq", down)
    gain = norm_gain.reshape(1, -1)
    turned = step_weight.T
    gate, mix, raw = project(
        hidden_in, gain, gate_weight, value_weight, state_weight, jnp.concatenate([turned, turned])
    )
    halo = jnp.concatenate([before, after])
    conv, fresh, cols, row, end, total = states(
        "seq",
        mix,
        halo,
        gain,
        value_weight,
        state_weight,
        raw,
        piece_lengths,
        step_bias,
        decay_log,
        conv_value,
        conv_state,
    )
    incoming, w_all = exchange((seq_count, head_count), end, total, output_weight)
    gf, gb, ss = outputs(conv, gate, cols, row, fresh, incoming, skip_gain)
    return finish(
        head_count, gf, gb, ss, output_gain.reshape(1, -1), hidden_in, output_weight, w_all
    )


def solution(mesh):
    in_specs = (
        P("seq", None),
        P(),
        P(None, "head"),
        P(None, "head"),
        P(),
        P(None, "head"),
        P("head"),
        P("head"),
        P("head"),
        P(None, "head"),
        P(),
        P("head"),
        P("head", None),
        P(),
    )
    out_specs = P(("seq", "head"), None)
    return jax.shard_map(local, mesh=mesh, in_specs=in_specs, out_specs=out_specs, check_vma=False)
```

profile of v0, /device:TPU:1, one launch (start us, length us, event | category | flops | bytes accessed | tf_op | source)
XLA Modules:
  0.0 159.8 jit_solution(8961354046004123561)
XLA Ops:
  0.0 0.7 fusion
  0.7 3.9 %collective-permute-start = (bf16[8,1024]{1,0:T(8,128)(2,1)S(1)}, bf16[8,1024]{1,0:T(8,128)(2,1)S(1)}, u32[]{:S(2)}, u32[]{:S(2)}) collective-permute-start(bf16[8,1024]{1,0:T(8,128)(2,1)S(1)} %get-tuple-element.33), channel_id=1, source_target_pairs={{0,8},{8,16},{16,24},{24,32},{32,40},{40,48},{48,56},{56,64},{64,7... | collective-permute-start | bytes 49160 | tf_op jit(solution)/shard_map/ppermute | solution.py:699
  4.7 1.3 collective-permute-start.1
  6.0 1.3 reshape.6.gain_ref
  7.2 1.4 pad_maximum_fusion.1.tw_ref
  8.6 0.0 copy-start
  8.6 14.1 %project.1 = (bf16[4096,256]{1,0:T(8,128)(2,1)}, bf16[4096,512]{1,0:T(8,128)(2,1)}, f32[32,8,128]{2,1,0:T(8,128)}) custom-call(bf16[4096,1024]{1,0:T(8,128)(2,1)} %hidden_ref.1, bf16[1,1024]{1,0:T(2,128)(2,1)} %reshape.6.gain_ref, bf16[1024,256]{1,0:T(8,128)(2,1)} %gw_ref.1, bf16[1024,256]{1,0:T(8,128)(2,1)} %vw_ref.3, bf16[1024,256]{1,0:T(8,128)(2,1)} %sw_ref.3, ...), custom_call_target="tpu_custom_call" | custom-call | flops 8589934592 | bytes 20971520 | tf_op jit(solution)/shard_map/project/pallas_call | solution.py:73
  22.7 0.0 copy-done
  22.7 0.6 reshape.7.gain_ref
  23.3 0.0 collective-permute-done
  23.3 0.0 collective-permute-done.1
  23.3 0.6 pad_maximum_fusion.halo_ref
  23.9 33.4 %states.1 = (bf16[4096,1024]{1,0:T(8,128)(2,1)}, bf16[32,2,128,256]{3,2,1,0:T(8,128)(2,1)}, f32[32,32,128]{2,1,0:T(8,128)}, f32[32,8,128]{2,1,0:T(8,128)}, bf16[...) custom-call(bf16[4096,512]{1,0:T(8,128)(2,1)} %get-tuple-element.19.mix_ref.before_ref.after_ref, ...), custom_call_target="tpu_custom_call" | custom-call | tf_op jit(solution)/shard_map/states/pallas_call | solution.py:269
  57.3 33.4 %exchange.1 = (f32[2,128,256]{2,1,0:T(8,128)}, bf16[8,256,1024]{2,1,0:T(8,128)(2,1)}) custom-call(bf16[2,128,256]{2,1,0:T(8,128)(2,1)} %get-tuple-element.26.end_ref, f32[8,256]{1,0:T(8,128)} %get-tuple-element.27.total_ref, bf16[256,1024]{1,0:T(8,128)(2,1)} %w_ref.3), custom_call_target="tpu_custom_call" | custom-call | tf_op jit(solution)/shard_map/exchange/pallas_call | solution.py:419
  90.7 27.5 %outputs.1 = (bf16[4096,256]{1,0:T(8,128)(2,1)}, bf16[4096,256]{1,0:T(8,128)(2,1)}, f32[64,128]{1,0:T(8,128)}) custom-call(bf16[4096,1024]{1,0:T(8,128)(2,1)} %get-tuple-element.21.conv_ref, bf16[4096,256]{1,0:T(8,128)(2,1)} %get-tuple-element.22.gate_ref, f32[32,32,128]{2,1,0:T(8,128)} %get-tuple-element.23.cols_ref, ...), custom_call_target="tpu_custom_call" | custom-call | tf_op jit(solution)/shard_map/outputs/pallas_call | solution.py:528
  118.2 39.3 %finish.1 = bf16[512,1024]{1,0:T(8,128)(2,1)} custom-call(bf16[4096,256]{1,0:T(8,128)(2,1)} %get-tuple-element.29.gf_ref, bf16[4096,256]{1,0:T(8,128)(2,1)} %get-tuple-element.30.gb_ref, f32[64,128]{1,0:T(8,128)} %get-tuple-element.31.ss_ref, bf16[1,256]{1,0:T(2,128)(2,1)} %reshape.7.gain_ref, bf16[4096,1024]{1,0:T(8,128)(2,1)} %hidden_ref.1, ...), custom_call_target="tpu_custom_call" | custom-call | tf_op jit(solution)/shard_map/finish/pallas_call | solution.py:650
  157.5 2.3 %copy.16 = bf16[512,1024]{1,0:T(8,128)(2,1)} copy(bf16[512,1024]{1,0:T(8,128)(2,1)} %finish.1) | data formatting | bytes 2097152
Async XLA Ops:
  0.7 22.5 %collective-permute-start = (bf16[8,1024]{1,0:T(8,128)(2,1)S(1)}, bf16[8,1024]{1,0:T(8,128)(2,1)S(1)}, u32[]{:S(2)}, u32[]{:S(2)}) collective-permute-start(bf16[8,1024]{1,0:T(8,128)(2,1)S(1)} %get-tuple-element.33), channel_id=1, source_target_pairs={{0,8},{8,16},{16,24},{24,32},{32,40},{40,48},{48,56},{56,64},{64,7... | collective-permute-start | bytes 49160 | tf_op jit(solution)/shard_map/ppermute | solution.py:699
  4.7 18.6 %collective-permute-start.1 = (bf16[8,1024]{1,0:T(8,128)(2,1)S(1)}, bf16[8,1024]{1,0:T(8,128)(2,1)S(1)}, u32[]{:S(2)}, u32[]{:S(2)}) collective-permute-start(bf16[8,1024]{1,0:T(8,128)(2,1)S(1)} %get-tuple-element.34), channel_id=1, source_target_pairs={{8,0},{16,8},{24,16},{32,24},{40,32},{48,40},{56,48},{64,56},{72,6... | collective-permute-start | bytes 49160 | tf_op jit(solution)/shard_map/ppermute | solution.py:700
  8.6 14.1 %copy-start = (bf16[256]{0:T(256)(128)(2,1)S(1)}, bf16[256]{0:T(256)(128)(2,1)}, u32[]{:S(2)}) copy-start(bf16[256]{0:T(256)(128)(2,1)} %param.25) | copy-start | bytes 1540
where the time goes:
time: 161 us; the launch traced here: 160 us
  Pallas kernels  148 us (92%)
  starting transfers between devices  5.21 us (3%)
  local copies, waits for them, and re-layouts  4.84 us (3%)
  other arithmetic  1.99 us (1%)
    pallas_call x1, Pallas kernels, finish(): pl.pallas_call(functools.partial(finish_kernel, head_count), in_specs=[wh...  39.3 us
    pallas_call x1, Pallas kernels, states(): pl.pallas_call(functools.partial(states_kernel, axis), grid=(chunks,), in...  33.4 us
    pallas_call x1, Pallas kernels, exchange(): pl.pallas_call(functools.partial(exchange_kernel, seq_count, head_count),...  33.4 us
    pallas_call x1, Pallas kernels, outputs(): pl.pallas_call(outputs_kernel, grid=(tokens // rows,), in_specs=[pl.Block...  27.5 us
    pallas_call x1, Pallas kernels, project(): pl.pallas_call(project_kernel, grid=(tokens // rows,), in_specs=[pl.Block...  14.1 us
    ppermute x1, starting transfers between devices, local(): before = lax.ppermute(hidden_in[-HALO:], 'seq', up)  3.92 us
  transfers between devices with their start and end apart: 2, of which 0 were waited for; matrix products, arithmetic and copies ran while one was open for 2% of the time, Pallas kernels for 9%

commit v1 on v0

--- a/solution.py
+++ b/solution.py
@@ -13,7 +13,8 @@
 CONV = 4
 CHUNK = 128
 PIECES = 16
-HALO = 8
+HALO = 16
+REACH = 8
 RESET = 256.0
 LOG2E = math.log2(math.e)
 
@@ -54,24 +55,112 @@
     return pltpu.CompilerParams(vmem_limit_bytes=60 * 1024 * 1024, **kw)
 
 
-def project_kernel(h_ref, gain_ref, gw_ref, vw_ref, sw_ref, tw_ref, gate_ref, mix_ref, raw_ref):
+def remote(src, dst, send, recv, **where):
+    return pltpu.make_async_remote_copy(
+        src_ref=src,
+        dst_ref=dst,
+        send_sem=send,
+        recv_sem=recv,
+        device_id=where,
+        device_id_type=MESH,
+    )
+
+
+def greet(axes_and_peers):
+    barrier = pltpu.get_barrier_semaphore()
+    for where in axes_and_peers:
+        pl.semaphore_signal(barrier, inc=1, device_id=where, device_id_type=MESH)
+    pl.semaphore_wait(barrier, len(axes_and_peers))
+
+
+def head_peer(me, chips, dy, dc):
+    y, core = me // 2, me % 2
+    return ((y + dy) % chips) * 2 + (core + dc) % 2
+
+
+def project_copies(seq_count, head_count, hidden, w, halo, hop, send, recv):
+    me = lax.axis_index("seq")
+    head = lax.axis_index("head")
+    chips = head_count // 2
+    tokens = hidden.shape[0]
+    after = (me + 1) % seq_count
+    before = (me + seq_count - 1) % seq_count
+    first, last = pl.ds(0, HALO), pl.ds(tokens - HALO, HALO)
+    low, high = pl.ds(0, HALO), pl.ds(HALO, HALO)
+    up = head_peer(head, chips, 1, 0)
+    down = head_peer(head, chips, chips - 1, 0)
+    partner = head_peer(head, chips, 0, 1)
+    return (
+        remote(hidden.at[last], halo.at[low], send.at[0], recv.at[0], seq=after),
+        remote(hidden.at[first], halo.at[high], send.at[1], recv.at[1], seq=before),
+        remote(w, hop.at[0], send.at[2], recv.at[2], head=up),
+        remote(w, hop.at[1], send.at[3], recv.at[3], head=down),
+        remote(w, hop.at[2], send.at[4], recv.at[4], head=partner),
+    ), [{"seq": after}, {"seq": before}, {"head": up}, {"head": down}, {"head": partner}]
+
+
+def project_kernel(
+    mesh_shape,
+    h_ref,
+    gain_ref,
+    gw_ref,
+    vw_ref,
+    sw_ref,
+    tw_ref,
+    hidden,
+    w,
+    gate_ref,
+    mix_ref,
+    raw_ref,
+    halo,
+    hop,
+    turned,
+    send,
+    recv,
+):
+    i = pl.program_id(0)
+    copies, peers = project_copies(*mesh_shape, hidden, w, halo, hop, send, recv)
+    barrier = pltpu.get_barrier_semaphore()
+
+    @pl.when(i == 0)
+    def _():
+        for where in peers:
+            pl.semaphore_signal(barrier, inc=1, device_id=where, device_id_type=MESH)
+        narrow = tw_ref[...].astype(f32)
+        depth, few = narrow.shape
+        padded = jnp.concatenate(
+            [narrow, narrow, jnp.zeros((depth, CHUNK - 2 * few), f32)], axis=1
+        )
+        turned[...] = padded.T[:8].astype(bf16)
+
+    @pl.when(i == 1)
+    def _():
+        pl.semaphore_wait(barrier, len(peers))
+        for copy in copies:
+            copy.start()
+
     inner = vw_ref.shape[1]
-    n = normalized(h_ref[...], gain_ref[...])
+    n = normalized(h_ref[...], gain_ref[...].reshape(1, -1))
     gate_ref[...] = mm(n, gw_ref[...]).astype(bf16)
     mix_ref[:, :inner] = mm(n, vw_ref[...]).astype(bf16)
     mix_ref[:, inner:] = mm(n, sw_ref[...]).astype(bf16)
-    raw = mm(tw_ref[...], n, NT)
+    raw = mm(turned[...], n, NT)
     for q in range(raw.shape[1] // CHUNK):
         raw_ref[q] = raw[:, q * CHUNK : (q + 1) * CHUNK]
 
-
-def project(hidden, gain, gw, vw, sw, tw):
+    @pl.when(i == pl.num_programs(0) - 1)
+    def _():
+        for copy in copies:
+            copy.wait()
+
+
+def project(mesh_shape, hidden, gain, gw, vw, sw, tw, w):
     tokens, width = hidden.shape
     inner = vw.shape[1]
     mixed = inner + sw.shape[1]
-    rows = 512
+    rows = min(512, tokens // 2)
     return pl.pallas_call(
-        project_kernel,
+        functools.partial(project_kernel, mesh_shape),
         grid=(tokens // rows,),
         in_specs=[
             pl.BlockSpec((rows, width), lambda i: (i, 0)),
@@ -80,23 +169,31 @@
             whole(vw.shape),
             whole(sw.shape),
             whole(tw.shape),
+            ANY_SPEC,
+            ANY_SPEC,
         ],
         out_specs=[
             pl.BlockSpec((rows, inner), lambda i: (i, 0)),
             pl.BlockSpec((rows, mixed), lambda i: (i, 0)),
             pl.BlockSpec((rows // CHUNK, 8, CHUNK), lambda i: (i, 0, 0)),
+            ANY_SPEC,
+            ANY_SPEC,
         ],
         out_shape=[
             jax.ShapeDtypeStruct((tokens, inner), bf16),
             jax.ShapeDtypeStruct((tokens, mixed), bf16),
             jax.ShapeDtypeStruct((tokens // CHUNK, 8, CHUNK), f32),
-        ],
-        compiler_params=params(),
-        cost_estimate=pl.CostEstimate(
-            flops=2 * tokens * width * 1024, bytes_accessed=20 << 20, transcendentals=0
-        ),
+            jax.ShapeDtypeStruct((2 * HALO, width), bf16),
+            jax.ShapeDtypeStruct((3,) + w.shape, bf16),
+        ],
+        scratch_shapes=[
+            pltpu.VMEM((8, width), bf16),
+            pltpu.SemaphoreType.DMA((5,)),
+            pltpu.SemaphoreType.DMA((5,)),
+        ],
+        compiler_params=params(collective_id=2, has_side_effects=True),
         name="project",
-    )(hidden, gain, gw, vw, sw, tw)
+    )(hidden, gain, gw, vw, sw, tw, hidden, w)
 
 
 def head_lanes(columns):
@@ -146,7 +243,7 @@
     ).reshape(shape)
     excl = cum - log
     total = cum[:, :, CHUNK - 1 :]
-    log_step = jnp.log2(step)
+    log_step = jnp.where(step > 0.0, jnp.log2(step), -RESET)
     row = jnp.where(upper, cum - log_step, excl + log_step)
     g1 = jnp.where(upper, cum, excl)
     g2 = jnp.where(upper, jnp.exp2(cum), jnp.exp2(total - cum) * step)
@@ -176,22 +273,25 @@
     row_ref,
     end_ref,
     total_ref,
-    ext,
+    prod,
     halo,
     run,
     reach,
+    spread,
+    near,
 ):
     c = pl.program_id(0)
     count = pl.num_programs(0)
     inner = vw_ref.shape[1]
     mixed = mix_ref.shape[1]
+    blocks = mixed // 128
+    first_row = lax.axis_index(axis) * (count * CHUNK)
 
     @pl.when(c == 0)
     def _():
-        n = normalized(halo_ref[...], gain_ref[...])
+        n = normalized(halo_ref[...], gain_ref[...].reshape(1, -1))
         halo[:, :inner] = mm(n, vw_ref[...]).astype(bf16).astype(f32)
         halo[:, inner:] = mm(n, sw_ref[...]).astype(bf16).astype(f32)
-        first_row = lax.axis_index(axis) * (count * CHUNK)
         row, g1, g2, g3, g4 = decays(first_row, raw_ref[...], lens_ref, bias_ref, rate_ref)
         row_ref[...] = row
         cols_ref[:, 0:8, :] = g1
@@ -200,52 +300,91 @@
         cols_ref[:, 24:32, :] = g4
         run[...] = jnp.zeros_like(run)
         reach[...] = jnp.zeros_like(reach)
-
-    ext[HALO : HALO + CHUNK, :] = mix_ref[...].astype(f32)
+        line = lax.broadcasted_iota(jnp.int32, spread.shape, 0) % 32
+        lane = lax.broadcasted_iota(jnp.int32, spread.shape, 1)
+        wanted = 12 + (lane // inner) * 8 + (lane % inner) // HEAD_DIM
+        spread[...] = (line == wanted).astype(f32).astype(bf16)
+
+        def clear(k, carry):
+            near[k] = 0
+            return carry
+
+        lax.fori_loop(0, near.shape[0], clear, 0)
+
+        def mark(k, edge):
+            for shift in (-(CONV - 1), CONV - 2):
+                at = (edge + shift - first_row + CHUNK) // CHUNK
+                near[jnp.clip(at, 0, near.shape[0] - 1)] = 1
+            return edge + lens_ref[jnp.minimum(k, PIECES - 1)]
+
+        lax.fori_loop(0, PIECES + 1, mark, jnp.int32(0))
+
+    taps = jnp.concatenate([cv_ref[...], cs_ref[...]], axis=1).astype(f32)
+    here = slice(REACH, REACH + CHUNK)
+
+    def put(rows, values):
+        for k in range(CONV - 1):
+            for b in range(blocks):
+                lanes = slice(b * 128, (b + 1) * 128)
+                prod[k, b, rows, :] = values[:, lanes] * taps[k : k + 1, lanes]
+
+    put(here, mix_ref[...].astype(f32))
+    ahead, behind = slice(0, REACH), slice(REACH + CHUNK, 2 * REACH + CHUNK)
 
     @pl.when(c == 0)
     def _():
-        ext[0:HALO, :] = halo[0:HALO, :]
+        put(ahead, halo[HALO - REACH : HALO, :])
 
     @pl.when(c > 0)
     def _():
-        ext[0:HALO, :] = before_ref[...].astype(f32)[HALO:, :]
+        put(ahead, before_ref[...].astype(f32)[16 - REACH :, :])
 
     @pl.when(c == count - 1)
     def _():
-        ext[HALO + CHUNK :, :] = halo[HALO:, :]
+        put(behind, halo[HALO : HALO + REACH, :])
 
     @pl.when(c < count - 1)
     def _():
-        ext[HALO + CHUNK :, :] = after_ref[...].astype(f32)[:HALO, :]
+        put(behind, after_ref[...].astype(f32)[:REACH, :])
 
     cols = cols_ref[c]
-    turned = jnp.concatenate([cols, jnp.zeros((CHUNK - 32, CHUNK), f32)], axis=0).T
-    width = 128
-    since = jnp.broadcast_to(turned[:, 24:25], (CHUNK, width))
-    until = jnp.broadcast_to(turned[:, 28:29], (CHUNK, width))
-    taps = jnp.concatenate([cv_ref[...], cs_ref[...]], axis=1).astype(f32)
-    for reverse in (False, True):
-        left = until if reverse else since
-        for block in range(mixed // width):
-            lanes = slice(block * width, (block + 1) * width)
-            total = ext[HALO : HALO + CHUNK, lanes] * taps[CONV - 1 : CONV, lanes]
-            for distance in range(1, CONV):
-                at = HALO + distance if reverse else HALO - distance
-                term = ext[at : at + CHUNK, lanes] * taps[CONV - 1 - distance : CONV - distance, lanes]
-                total = total + jnp.where(left >= distance, term, 0.0)
-            base = mixed if reverse else 0
-            conv_ref[:, base + block * width : base + (block + 1) * width] = silu(total).astype(bf16)
-
-    tails = (
-        head_lanes([turned[:, 12 + h : 13 + h] for h in range(4)]),
-        head_lanes([turned[:, 20 + h : 21 + h] for h in range(4)]),
-    )
+
+    def convolve(masked):
+        if masked:
+            turned = jnp.concatenate([cols, jnp.zeros((CHUNK - 32, CHUNK), f32)], axis=0).T
+            sides = [jnp.broadcast_to(turned[:, r : r + 1], (CHUNK, 128)) for r in (24, 28)]
+        for b in range(blocks):
+            lanes = slice(b * 128, (b + 1) * 128)
+            centre = mix_ref[:, lanes].astype(f32) * taps[CONV - 1 : CONV, lanes]
+            for d in range(2):
+                total = centre
+                for distance in range(1, CONV):
+                    at = REACH + distance if d else REACH - distance
+                    term = prod[CONV - 1 - distance, b, at : at + CHUNK, :]
+                    if masked:
+                        term = jnp.where(sides[d] >= distance, term, 0.0)
+                    total = total + term
+                at = d * mixed + b * 128
+                conv_ref[:, at : at + 128] = silu(total).astype(bf16)
+
+    edges = near[c + 1]
+
+    @pl.when(edges == 0)
+    def _():
+        convolve(False)
+
+    @pl.when(edges != 0)
+    def _():
+        convolve(True)
+
+    high = cols.astype(bf16).astype(f32)
+    both = jnp.concatenate([high, cols - high], axis=0).astype(bf16)
+    tails = mm(both, spread[...], TN)
     passing = head_lanes([cols[h : h + 1, CHUNK - 1 :] for h in range(4)])
     for d in range(2):
         x = conv_ref[:, d * mixed : d * mixed + inner].astype(f32)
         write = conv_ref[:, d * mixed + inner : d * mixed + inner + STATE]
-        scaled = (x * tails[d]).astype(bf16)
+        scaled = (x * tails[:, d * inner : (d + 1) * inner]).astype(bf16)
         fresh = mm(write, scaled, TN)
         fresh_ref[0, d] = fresh.astype(bf16)
         if d == 0:
@@ -301,37 +440,16 @@
             jax.ShapeDtypeStruct((8, inner), f32),
         ],
         scratch_shapes=[
-            pltpu.VMEM((CHUNK + 2 * HALO, mixed), f32),
+            pltpu.VMEM((CONV - 1, mixed // 128, CHUNK + 2 * REACH, 128), f32),
             pltpu.VMEM((2 * HALO, mixed), f32),
             pltpu.VMEM((2, STATE, inner), f32),
             pltpu.VMEM((8, inner), f32),
+            pltpu.VMEM((64, 2 * inner), bf16),
+            pltpu.SMEM((chunks + 2,), jnp.int32),
         ],
         compiler_params=params(),
         name="states",
     )(mix, mix, mix, halo, gain, vw, sw, raw, lens, bias, rate, cv, cs)
-
-
-def remote(src, dst, send, recv, **where):
-    return pltpu.make_async_remote_copy(
-        src_ref=src,
-        dst_ref=dst,
-        send_sem=send,
-        recv_sem=recv,
-        device_id=where,
-        device_id_type=MESH,
-    )
-
-
-def greet(axes_and_peers):
-    barrier = pltpu.get_barrier_semaphore()
-    for where in axes_and_peers:
-        pl.semaphore_signal(barrier, inc=1, device_id=where, device_id_type=MESH)
-    pl.semaphore_wait(barrier, len(axes_and_peers))
-
-
-def head_peer(me, chips, dy, dc):
-    y, core = me // 2, me % 2
-    return ((y + dy) % chips) * 2 + (core + dc) % 2
 
 
 def exchange_kernel(
@@ -339,9 +457,9 @@
     head_count,
     end_ref,
     total_ref,
-    w_ref,
+    hop_ref,
     in_ref,
-    all_ref,
+    far_ref,
     ends,
     totals,
     end_send,
@@ -354,7 +472,7 @@
     me = lax.axis_index("seq")
     head = lax.axis_index("head")
     chips = head_count // 2
-    half = w_ref.shape[0] // 2
+    half = hop_ref.shape[1] // 2
     up = head_peer(head, chips, 1, 0)
     down = head_peer(head, chips, chips - 1, 0)
     partner = head_peer(head, chips, 0, 1)
@@ -369,25 +487,22 @@
         started.append(copy)
         return copy
 
-    near = start(remote(w_ref, all_ref.at[2], w_send.at[0], w_recv.at[0], head=up))
-    far = start(remote(w_ref, all_ref.at[6], w_send.at[1], w_recv.at[1], head=down))
-    beside = start(remote(w_ref, all_ref.at[1], w_send.at[2], w_recv.at[2], head=partner))
+    top, bottom = pl.ds(0, half), pl.ds(half, half)
+    t1 = start(remote(hop_ref.at[0, top], far_ref.at[2, top], w_send.at[0], w_recv.at[0], head=up))
+    t3 = start(
+        remote(hop_ref.at[1, bottom], far_ref.at[2, bottom], w_send.at[1], w_recv.at[1], head=down)
+    )
+    t2 = start(remote(hop_ref.at[0], far_ref.at[0], w_send.at[2], w_recv.at[2], head=partner))
+    t4 = start(remote(hop_ref.at[1], far_ref.at[1], w_send.at[3], w_recv.at[3], head=partner))
     for k in range(1, seq_count):
         target = (me + k) % seq_count
         backward = (me + k) // seq_count
         start(remote(end_ref.at[backward], ends.at[k], end_send.at[k], end_recv.at[k], seq=target))
         start(remote(total_ref, totals.at[k], total_send.at[k], total_recv.at[k], seq=target))
 
-    near.wait_recv()
-    top, bottom = pl.ds(0, half), pl.ds(half, half)
-    t1 = start(remote(all_ref.at[2, top], all_ref.at[4, top], w_send.at[3], w_recv.at[3], head=up))
-    t2 = start(remote(all_ref.at[2], all_ref.at[3], w_send.at[4], w_recv.at[4], head=partner))
-    far.wait_recv()
-    t3 = start(
-        remote(all_ref.at[6, bottom], all_ref.at[4, bottom], w_send.at[5], w_recv.at[5], head=down)
-    )
-    t4 = start(remote(all_ref.at[6], all_ref.at[7], w_send.at[6], w_recv.at[6], head=partner))
-
+    t1.wait_recv()
+    t3.wait_recv()
+    t5 = start(remote(far_ref.at[2], far_ref.at[3], w_send.at[4], w_recv.at[4], head=partner))
     for k in range(1, seq_count):
         target = (me + k) % seq_count
         remote(end_ref.at[0], ends.at[k], end_send.at[k], end_recv.at[k], seq=target).wait_recv()
@@ -405,16 +520,13 @@
         def _(k=k):
             in_ref[1] = in_ref[1] * jnp.exp2(totals[k, 0:1, :]) + ends[k].astype(f32)
 
-    t1.wait_recv()
-    t3.wait_recv()
-    t5 = start(remote(all_ref.at[4], all_ref.at[5], w_send.at[7], w_recv.at[7], head=partner))
-    for copy in (beside, t2, t4, t5):
+    for copy in (t2, t4, t5):
         copy.wait_recv()
     for copy in started:
         copy.wait_send()
 
 
-def exchange(mesh_shape, end, total, w):
+def exchange(mesh_shape, end, total, hop):
     seq_count, head_count = mesh_shape
     return pl.pallas_call(
         functools.partial(exchange_kernel, seq_count, head_count),
@@ -422,7 +534,7 @@
         out_specs=[whole(end.shape), ANY_SPEC],
         out_shape=[
             jax.ShapeDtypeStruct(end.shape, f32),
-            jax.ShapeDtypeStruct((head_count,) + w.shape, bf16),
+            jax.ShapeDtypeStruct((4,) + hop.shape[1:], bf16),
         ],
         scratch_shapes=[
             pltpu.VMEM((seq_count,) + end.shape[1:], bf16),
@@ -431,16 +543,24 @@
             pltpu.SemaphoreType.DMA((seq_count,)),
             pltpu.SemaphoreType.DMA((seq_count,)),
             pltpu.SemaphoreType.DMA((seq_count,)),
-            pltpu.SemaphoreType.DMA((8,)),
-            pltpu.SemaphoreType.DMA((8,)),
+            pltpu.SemaphoreType.DMA((5,)),
+            pltpu.SemaphoreType.DMA((5,)),
         ],
         compiler_params=params(collective_id=0, has_side_effects=True),
         name="exchange",
-    )(end, total, w)
+    )(end, total, hop)
+
+
+def split(x, parts):
+    pieces = []
+    for _ in range(parts - 1):
+        pieces.append(x.astype(bf16).astype(f32))
+        x = x - pieces[-1]
+    return pieces + [x]
 
 
 def outputs_kernel(
-    conv_ref, gate_ref, cols_ref, row_ref, fresh_ref, in_ref, skip_ref, gf_ref, gb_ref, ss_ref, entry
+    conv_ref, gate_ref, cols_ref, row_ref, fresh_ref, in_ref, skip_ref, gf_ref, gb_ref, ss_ref, entry, pick
 ):
     g = pl.program_id(0)
     chunks = fresh_ref.shape[0]
@@ -464,6 +584,16 @@
 
         lax.fori_loop(0, chunks, forward, in_ref[0])
         lax.fori_loop(0, chunks, backward, in_ref[1])
+        line = lax.broadcasted_iota(jnp.int32, pick.shape[1:], 0)
+        lane = lax.broadcasted_iota(jnp.int32, pick.shape[1:], 1)
+        block = lane // CHUNK
+        sign = jnp.where(block < 4, 1.0, -1.0)
+        spot = lane - 8 * CHUNK
+        wanted = (spot // inner) * 8 + (spot % inner) // HEAD_DIM
+        chosen = jnp.where((line < 24) & (block < 8) & (line % 8 == block), sign, 0.0)
+        opened = (line >= 64) & (block >= 8) & (line % 16 == wanted)
+        for q in range(group):
+            pick[q] = jnp.where(opened, 1.0, chosen).astype(bf16)
 
     i = lax.broadcasted_iota(jnp.int32, (CHUNK, CHUNK), 0)
     j = lax.broadcasted_iota(jnp.int32, (CHUNK, CHUNK), 1)
@@ -478,8 +608,20 @@
         c = g * group + q
         rows = slice(q * CHUNK, (q + 1) * CHUNK)
         cols = cols_ref[c]
-        turned = jnp.concatenate([cols, jnp.zeros((CHUNK - 32, CHUNK), f32)], axis=0).T
         row = row_ref[c]
+        lines = jnp.concatenate(split(jnp.where(sub < 4, -row, row), 3), axis=0)
+        for block in range(8):
+            own = lax.broadcasted_iota(jnp.int32, lines.shape, 0) % 8 == block
+            pick[q, 32:56, block * CHUNK : (block + 1) * CHUNK] = jnp.where(own, lines, 0.0).astype(
+                bf16
+            )
+        left = jnp.concatenate(
+            split(cols[0:8], 3)
+            + [jnp.zeros((8, CHUNK), f32), jnp.ones((24, CHUNK), f32), jnp.zeros((8, CHUNK), f32)]
+            + split(cols[8:24], 2),
+            axis=0,
+        ).astype(bf16)
+        made = mm(left, pick[q], TN)
         pair = []
         for d, keep in ((0, lower), (1, upper)):
             base = d * mixed + inner
@@ -490,14 +632,13 @@
         for h in range(4):
             arg = jnp.where(
                 lower,
-                turned[:, h : h + 1] - row[h : h + 1, :],
-                row[4 + h : 5 + h, :] - turned[:, 4 + h : 5 + h],
+                made[:, h * CHUNK : (h + 1) * CHUNK],
+                made[:, (4 + h) * CHUNK : (5 + h) * CHUNK],
             )
             table = jnp.exp2(arg)
             for d in range(2):
                 weights[d].append((pair[d] * table).astype(bf16))
         gate = silu(gate_ref[rows, :].astype(f32))
-        opening = (8, 16)
         for d, out_ref in ((0, gf_ref), (1, gb_ref)):
             x = conv_ref[rows, d * mixed : d * mixed + inner]
             read = conv_ref[rows, d * mixed + inner + STATE : (d + 1) * mixed]
@@ -511,8 +652,8 @@
                 both = jnp.concatenate(weights[d][2 * p : 2 * p + 2], axis=1)
                 local.append(mm(both, stacked))
             carried = mm(read, entry[d, c])
-            open_at = opening[d]
-            scale = head_lanes([turned[:, open_at + h : open_at + h + 1] for h in range(4)])
+            at = 8 * CHUNK + d * inner
+            scale = made[:, at : at + inner]
             out = jnp.concatenate(local, axis=1) + carried * scale + skip * x.astype(f32)
             gated = out * gate
             out_ref[rows, :] = gated.astype(bf16)
@@ -547,7 +688,10 @@
             jax.ShapeDtypeStruct((tokens, inner), bf16),
             jax.ShapeDtypeStruct((2 * chunks, CHUNK), f32),
         ],
-        scratch_shapes=[pltpu.VMEM((2, chunks, STATE, inner), bf16)],
+        scratch_shapes=[
+            pltpu.VMEM((2, chunks, STATE, inner), bf16),
+            pltpu.VMEM((4, 96, 8 * CHUNK + 2 * inner), bf16),
+        ],
         compiler_params=params(),
         name="outputs",
     )(conv, gate, cols, row, fresh, incoming, skip)
@@ -561,7 +705,8 @@
     gain_ref,
     hidden_ref,
     w_ref,
-    all_ref,
+    hop_ref,
+    far_ref,
     out_ref,
     sums,
     sending,
@@ -576,7 +721,7 @@
 ):
     me = lax.axis_index("head")
     chips = head_count // 2
-    inner = gain_ref.shape[1]
+    inner = gain_ref.shape[0]
     rows = out_ref.shape[0]
     lines = ss_ref.shape[0] // head_count
     slots = [(dy, dc) for dy in range(chips) for dc in range(2)]
@@ -597,7 +742,7 @@
     for k in range(1, head_count):
         squares = squares + sums[k]
     total[...] = lax.rsqrt(squares * (1.0 / (inner * head_count)) + epsilon)
-    gain = gain_ref[...].astype(f32)
+    gain = gain_ref[...].reshape(1, -1).astype(f32)
 
     def combine(owner, slot):
         scale = total[pl.ds(pl.multiple_of(owner * lines, lines), lines), :]
@@ -628,13 +773,23 @@
             else:
                 rest_wide[:, lanes] = rest_wide[:, lanes] + term
 
+    held = {
+        1: hop_ref.at[2],
+        2: hop_ref.at[0],
+        3: far_ref.at[0],
+        head_count - 2: hop_ref.at[1],
+        head_count - 1: far_ref.at[1],
+        4: far_ref.at[2],
+        5: far_ref.at[3],
+    }
+
     def body(rest_wide_ref):
         nonlocal rest_wide
         rest_wide = rest_wide_ref
         add(sending[0], w_ref[...], True)
         for copy, k in reversed(list(zip(copies, order))):
             copy.wait_recv()
-            add(arrived[k], all_ref[k], False)
+            add(arrived[k], held[k], False)
         out_ref[...] = rest_wide_ref[...].astype(bf16)
 
     rest_wide = None
@@ -643,7 +798,7 @@
         copy.wait_send()
 
 
-def finish(head_count, gf, gb, ss, gain, hidden, w, w_all):
+def finish(head_count, gf, gb, ss, gain, hidden, w, hop, far):
     tokens, inner = gf.shape
     rows = tokens // head_count
     width = hidden.shape[1]
@@ -656,7 +811,8 @@
             whole(gain.shape),
             ANY_SPEC,
             whole(w.shape),
-            whole(w_all.shape),
+            whole(hop.shape),
+            whole(far.shape),
         ],
         out_specs=whole((rows, width)),
         out_shape=jax.ShapeDtypeStruct((rows, width), bf16),
@@ -674,7 +830,7 @@
         ],
         compiler_params=params(collective_id=1, has_side_effects=True),
         name="finish",
-    )(gf, gb, ss, gain, hidden, w, w_all)
+    )(gf, gb, ss, gain, hidden, w, hop, far)
 
 
 def local(
@@ -694,21 +850,15 @@
     piece_lengths,
 ):
     seq_count, head_count = lax.axis_size("seq"), lax.axis_size("head")
-    up = [(i, i + 1) for i in range(seq_count - 1)]
-    down = [(j, i) for i, j in up]
-    before = lax.ppermute(hidden_in[-HALO:], "seq", up)
-    after = lax.ppermute(hidden_in[:HALO], "seq", down)
-    gain = norm_gain.reshape(1, -1)
-    turned = step_weight.T
-    gate, mix, raw = project(
-        hidden_in, gain, gate_weight, value_weight, state_weight, jnp.concatenate([turned, turned])
+    shape = (seq_count, head_count)
+    gate, mix, raw, halo, hop = project(
+        shape, hidden_in, norm_gain, gate_weight, value_weight, state_weight, step_weight, output_weight
     )
-    halo = jnp.concatenate([before, after])
     conv, fresh, cols, row, end, total = states(
         "seq",
         mix,
         halo,
-        gain,
+        norm_gain,
         value_weight,
         state_weight,
         raw,
@@ -718,11 +868,9 @@
         conv_value,
         conv_state,
     )
-    incoming, w_all = exchange((seq_count, head_count), end, total, output_weight)
+    incoming, far = exchange(shape, end, total, hop)
     gf, gb, ss = outputs(conv, gate, cols, row, fresh, incoming, skip_gain)
-    return finish(
-        head_count, gf, gb, ss, output_gain.reshape(1, -1), hidden_in, output_weight, w_all
-    )
+    return finish(head_count, gf, gb, ss, output_gain, hidden_in, output_weight, hop, far)
 
 
 def solution(mesh):

time: 161 us -> 152 us (0.944)
  starting transfers between devices: 5.21 us -> 0 us
  other arithmetic: 1.99 us -> 0 us
    pallas_call x1, Pallas kernels: 33.4 us -> 18.7 us  [exchange(): pl.pallas_call(functools.partial(exchange_kernel, seq_count, head_count),...]
    pallas_call x1, Pallas kernels: 14.1 us -> 24 us  [project(): pl.pallas_call(functools.partial(project_kernel, mesh_shape), grid=(token...]
    ppermute x2 -> x0, starting transfers between devices: 5.21 us -> none  [the longest x1 3.92 us: local(): before = lax.ppermute(hidden_in[-HALO:], 'seq', up)]
    pallas_call x1, Pallas kernels: 27.5 us -> 32.1 us  [outputs(): pl.pallas_call(outputs_kernel, grid=(tokens // rows,), in_specs=[pl.Block...]
    concatenate x2 -> x0, other arithmetic: 1.99 us -> none  [the longest x1 1.39 us: local(): jnp.concatenate([turned, turned])]
    reshape x2 -> x0, local copies, waits for them, and re-layouts: 1.83 us -> none  [the longest x1 1.26 us: local(): gain = norm_gain.reshape(1, -1)]
    unnamed x3 -> x2, local copies, waits for them, and re-layouts: 2.27 us -> 3.84 us
  transfers between devices with their start and end apart: 2 -> 0, of which waited for: 0 -> 0; matrix products, arithmetic and copies ran while one was open for 2% -> 0% of each run, Pallas kernels for 9% -> 0%
where the time goes in v1:
time: 152 us; the launch traced here: 151 us
  Pallas kernels  147 us (97%)
  local copies, waits for them, and re-layouts  3.84 us (3%)
    pallas_call x1, Pallas kernels, finish(): pl.pallas_call(functools.partial(finish_kernel, head_count), in_specs=[wh...  40.3 us
    pallas_call x1, Pallas kernels, states(): pl.pallas_call(functools.partial(states_kernel, axis), grid=(chunks,), in...  32.2 us
    pallas_call x1, Pallas kernels, outputs(): pl.pallas_call(outputs_kernel, grid=(tokens // rows,), in_specs=[pl.Block...  32.1 us
    pallas_call x1, Pallas kernels, project(): pl.pallas_call(functools.partial(project_kernel, mesh_shape), grid=(token...  24 us
    pallas_call x1, Pallas kernels, exchange(): pl.pallas_call(functools.partial(exchange_kernel, seq_count, head_count),...  18.7 us
    unnamed x2, local copies, waits for them, and re-layouts  3.84 us

profile of v1, /device:TPU:1, one launch (start us, length us, event | category | flops | bytes accessed | tf_op | source)
XLA Modules:
  0.0 151.2 jit_solution(14821036715351555656)
XLA Ops:
  0.0 1.6 %copy.15.tw_ref = bf16[1024,4]{1,0:T(8,128)(2,1)} copy(bf16[1024,4]{0,1:T(4,128)(2,1)} %param.19) | data formatting | bytes 16384 | tf_op args[5]
  1.6 24.0 %project.1 = (bf16[4096,256]{1,0:T(8,128)(2,1)}, bf16[4096,512]{1,0:T(8,128)(2,1)}, f32[32,8,128]{2,1,0:T(8,128)}, bf16[32,1024]{1,0:T(8,128)(2,1)}, bf16[3,256,1024]{2,1,0:T(8,128)(2,1)}) custom-call(bf16[4096,1024]{1,0:T(8,128)(2,1)} %hidden_ref.1, bf16[1024]{0:T(1024)(128)(2,1)} %gain_ref.4, bf16[1024,256]{1,0:T(8,128)(2,1)} %gw_ref.1, ...), custom_call_target="tpu_custom_call" | custom-call | tf_op jit(solution)/shard_map/project/pallas_call | solution.py:162
  25.5 32.2 %states.1 = (bf16[4096,1024]{1,0:T(8,128)(2,1)}, bf16[32,2,128,256]{3,2,1,0:T(8,128)(2,1)}, f32[32,32,128]{2,1,0:T(8,128)}, f32[32,8,128]{2,1,0:T(8,128)}, bf16[...) custom-call(bf16[4096,512]{1,0:T(8,128)(2,1)} %get-tuple-element.21.mix_ref.before_ref.after_ref, ...), custom_call_target="tpu_custom_call" | custom-call | tf_op jit(solution)/shard_map/states/pallas_call | solution.py:408
  57.8 18.7 %exchange.1 = (f32[2,128,256]{2,1,0:T(8,128)}, bf16[4,256,1024]{2,1,0:T(8,128)(2,1)}) custom-call(bf16[2,128,256]{2,1,0:T(8,128)(2,1)} %get-tuple-element.29.end_ref, f32[8,256]{1,0:T(8,128)} %get-tuple-element.30.total_ref, bf16[3,256,1024]{2,1,0:T(8,128)(2,1)} %get-tuple-element.31.hop_ref), custom_call_target="tpu_custom_call" | custom-call | tf_op jit(solution)/shard_map/exchange/pallas_call | solution.py:531
  76.5 32.1 %outputs.1 = (bf16[4096,256]{1,0:T(8,128)(2,1)}, bf16[4096,256]{1,0:T(8,128)(2,1)}, f32[64,128]{1,0:T(8,128)}) custom-call(bf16[4096,1024]{1,0:T(8,128)(2,1)} %get-tuple-element.24.conv_ref, bf16[4096,256]{1,0:T(8,128)(2,1)} %get-tuple-element.25.gate_ref, f32[32,32,128]{2,1,0:T(8,128)} %get-tuple-element.26.cols_ref, ...), custom_call_target="tpu_custom_call" | custom-call | tf_op jit(solution)/shard_map/outputs/pallas_call | solution.py:669
  108.6 40.3 %finish.1 = bf16[512,1024]{1,0:T(8,128)(2,1)} custom-call(bf16[4096,256]{1,0:T(8,128)(2,1)} %get-tuple-element.33.gf_ref, bf16[4096,256]{1,0:T(8,128)(2,1)} %get-tuple-element.34.gb_ref, f32[64,128]{1,0:T(8,128)} %get-tuple-element.35.ss_ref, bf16[256]{0:T(256)(128)(2,1)} %gain_ref.5, bf16[4096,1024]{1,0:T(8,128)(2,1)} %hidden_ref.1, ...), custom_call_target="tpu_custom_call" | custom-call | tf_op jit(solution)/shard_map/finish/pallas_call | solution.py:805
  148.9 2.3 %copy.17 = bf16[512,1024]{1,0:T(8,128)(2,1)} copy(bf16[512,1024]{1,0:T(8,128)(2,1)} %finish.1) | data formatting | bytes 2097152

commit v2 on v1

v2 whole, which is shorter than its diff:
```python
import functools
import math

import jax
import jax.numpy as jnp
from jax import lax
from jax.experimental import pallas as pl
from jax.experimental.pallas import tpu as pltpu
from jax.sharding import PartitionSpec as P

HEAD_DIM = 64
STATE = 128
CONV = 4
CHUNK = 128
PIECES = 16
HALO = 16
REACH = 8
RESET = 256.0
LOG2E = math.log2(math.e)

f32 = jnp.float32
bf16 = jnp.bfloat16
epsilon = 1e-05
MESH = pl.DeviceIdType.MESH
NN = (((1,), (0,)), ((), ()))
NT = (((1,), (1,)), ((), ()))
TN = (((0,), (0,)), ((), ()))


def mm(a, b, dims=NN, precision=None):
    return lax.dot_general(a, b, dims, precision=precision, preferred_element_type=f32)


def silu(x):
    half = 0.5 * x
    return half * jnp.tanh(half) + half


def normalized(h, gain):
    wide = h.astype(f32)
    scale = lax.rsqrt(jnp.mean(wide * wide, axis=1, keepdims=True) + epsilon)
    return (wide * scale * gain.astype(f32)).astype(bf16)


def whole(shape):
    zeros = (0,) * len(shape)
    return pl.BlockSpec(shape, lambda *_: zeros)


SMEM_SPEC = pl.BlockSpec(memory_space=pltpu.SMEM)
ANY_SPEC = pl.BlockSpec(memory_space=pl.ANY)


def params(**kw):
    return pltpu.CompilerParams(vmem_limit_bytes=60 * 1024 * 1024, **kw)


def remote(src, dst, send, recv, **where):
    return pltpu.make_async_remote_copy(
        src_ref=src,
        dst_ref=dst,
        send_sem=send,
        recv_sem=recv,
        device_id=where,
        device_id_type=MESH,
    )


def greet(axes_and_peers):
    barrier = pltpu.get_barrier_semaphore()
    for where in axes_and_peers:
        pl.semaphore_signal(barrier, inc=1, device_id=where, device_id_type=MESH)
    pl.semaphore_wait(barrier, len(axes_and_peers))


def head_peer(me, chips, dy, dc):
    y, core = me // 2, me % 2
    return ((y + dy) % chips) * 2 + (core + dc) % 2


def project_copies(seq_count, head_count, hidden, w, halo, hop, send, recv):
    me = lax.axis_index("seq")
    head = lax.axis_index("head")
    chips = head_count // 2
    tokens = hidden.shape[0]
    after = (me + 1) % seq_count
    before = (me + seq_count - 1) % seq_count
    first, last = pl.ds(0, HALO), pl.ds(tokens - HALO, HALO)
    low, high = pl.ds(0, HALO), pl.ds(HALO, HALO)
    up = head_peer(head, chips, 1, 0)
    down = head_peer(head, chips, chips - 1, 0)
    partner = head_peer(head, chips, 0, 1)
    return (
        remote(hidden.at[last], halo.at[low], send.at[0], recv.at[0], seq=after),
        remote(hidden.at[first], halo.at[high], send.at[1], recv.at[1], seq=before),
        remote(w, hop.at[0], send.at[2], recv.at[2], head=up),
        remote(w, hop.at[1], send.at[3], recv.at[3], head=down),
        remote(w, hop.at[2], send.at[4], recv.at[4], head=partner),
    ), [{"seq": after}, {"seq": before}, {"head": up}, {"head": down}, {"head": partner}]


def project_kernel(
    mesh_shape,
    h_ref,
    gain_ref,
    gw_ref,
    vw_ref,
    sw_ref,
    tw_ref,
    hidden,
    w,
    gate_ref,
    mix_ref,
    raw_ref,
    halo,
    hop,
    turned,
    send,
    recv,
):
    i = pl.program_id(0)
    copies, peers = project_copies(*mesh_shape, hidden, w, halo, hop, send, recv)
    barrier = pltpu.get_barrier_semaphore()

    @pl.when(i == 0)
    def _():
        for where in peers:
            pl.semaphore_signal(barrier, inc=1, device_id=where, device_id_type=MESH)
        narrow = tw_ref[...].astype(f32)
        depth, few = narrow.shape
        padded = jnp.concatenate(
            [narrow, narrow, jnp.zeros((depth, CHUNK - 2 * few), f32)], axis=1
        )
        turned[...] = padded.T[:8].astype(bf16)

    @pl.when(i == 1)
    def _():
        pl.semaphore_wait(barrier, len(peers))
        for copy in copies:
            copy.start()

    inner = vw_ref.shape[1]
    n = normalized(h_ref[...], gain_ref[...].reshape(1, -1))
    gate = mm(n, gw_ref[...]).astype(bf16)
    for q in range(gate_ref.shape[0]):
        gate_ref[q, 0] = gate[q * CHUNK : (q + 1) * CHUNK]
    mix_ref[:, :inner] = mm(n, vw_ref[...]).astype(bf16)
    mix_ref[:, inner:] = mm(n, sw_ref[...]).astype(bf16)
    raw = mm(turned[...], n, NT)
    for q in range(raw.shape[1] // CHUNK):
        raw_ref[q] = raw[:, q * CHUNK : (q + 1) * CHUNK]

    @pl.when(i == pl.num_programs(0) - 1)
    def _():
        for copy in copies:
            copy.wait()


def project(mesh_shape, hidden, gain, gw, vw, sw, tw, w):
    tokens, width = hidden.shape
    inner = vw.shape[1]
    mixed = inner + sw.shape[1]
    rows = tokens // mesh_shape[1]
    rounds = rows // CHUNK
    return pl.pallas_call(
        functools.partial(project_kernel, mesh_shape),
        grid=(tokens // rows,),
        in_specs=[
            pl.BlockSpec((rows, width), lambda i: (i, 0)),
            whole(gain.shape),
            whole(gw.shape),
            whole(vw.shape),
            whole(sw.shape),
            whole(tw.shape),
            ANY_SPEC,
            ANY_SPEC,
        ],
        out_specs=[
            pl.BlockSpec((rounds, 1, CHUNK, inner), lambda i: (0, i, 0, 0)),
            pl.BlockSpec((rows, mixed), lambda i: (i, 0)),
            pl.BlockSpec((rows // CHUNK, 8, CHUNK), lambda i: (i, 0, 0)),
            ANY_SPEC,
            ANY_SPEC,
        ],
        out_shape=[
            jax.ShapeDtypeStruct((rounds, tokens // rows, CHUNK, inner), bf16),
            jax.ShapeDtypeStruct((tokens, mixed), bf16),
            jax.ShapeDtypeStruct((tokens // CHUNK, 8, CHUNK), f32),
            jax.ShapeDtypeStruct((2 * HALO, width), bf16),
            jax.ShapeDtypeStruct((3,) + w.shape, bf16),
        ],
        scratch_shapes=[
            pltpu.VMEM((8, width), bf16),
            pltpu.SemaphoreType.DMA((5,)),
            pltpu.SemaphoreType.DMA((5,)),
        ],
        compiler_params=params(collective_id=2, has_side_effects=True),
        name="project",
    )(hidden, gain, gw, vw, sw, tw, hidden, w)


def head_lanes(columns):
    low = lax.broadcasted_iota(jnp.int32, (columns[0].shape[0], 2 * HEAD_DIM), 1) < HEAD_DIM
    pairs = [
        jnp.where(low, columns[2 * p], columns[2 * p + 1]) for p in range(len(columns) // 2)
    ]
    return jnp.concatenate(pairs, axis=1)


def decays(first_row, raw, lens_ref, bias_ref, rate_ref):
    chunks = raw.shape[0]
    shape = (chunks, 8, CHUNK)
    sub = lax.broadcasted_iota(jnp.int32, shape, 1)
    upper = sub < 4
    head = jnp.where(upper, sub, sub - 4)
    pos = (
        first_row
        + lax.broadcasted_iota(jnp.int32, shape, 0) * CHUNK
        + lax.broadcasted_iota(jnp.int32, shape, 2)
    )
    start = jnp.zeros(shape, jnp.int32)
    stop = jnp.full(shape, 1 << 30, jnp.int32)
    edge = jnp.int32(0)
    for k in range(PIECES):
        start = jnp.where(pos >= edge, edge, start)
        edge = edge + lens_ref[k]
        stop = jnp.minimum(stop, jnp.where(edge > pos, edge, 1 << 30))
    since = pos - start
    until = stop - 1 - pos
    bias = jnp.zeros(shape, f32)
    rate = jnp.zeros(shape, f32)
    for h in range(4):
        bias = jnp.where(head == h, bias_ref[h], bias)
        rate = jnp.where(head == h, rate_ref[h], rate)
    rate = jnp.exp(rate) * (-LOG2E)
    z = raw + bias
    step = jnp.maximum(z, 0.0) + jnp.log1p(jnp.exp(-jnp.abs(z)))
    log = step * rate
    reset = jnp.where(since == 0, -RESET, 0.0)
    ones = (
        lax.broadcasted_iota(jnp.int32, (CHUNK, CHUNK), 0)
        <= lax.broadcasted_iota(jnp.int32, (CHUNK, CHUNK), 1)
    ).astype(f32)
    cum = mm(
        (log + reset).reshape(chunks * 8, CHUNK), ones, precision=lax.Precision.HIGHEST
    ).reshape(shape)
    excl = cum - log
    total = cum[:, :, CHUNK - 1 :]
    log_step = jnp.where(step > 0.0, jnp.log2(step), -RESET)
    row = jnp.where(upper, cum - log_step, excl + log_step)
    g1 = jnp.where(upper, cum, excl)
    g2 = jnp.where(upper, jnp.exp2(cum), jnp.exp2(total - cum) * step)
    g3 = jnp.where(upper, jnp.exp2(total - excl), jnp.exp2(excl) * step)
    g4 = jnp.where(upper, since, until).astype(f32)
    return row, g1, g2, g3, g4


def states_kernel(
    axis,
    mix_ref,
    before_ref,
    after_ref,
    halo_ref,
    gain_ref,
    vw_ref,
    sw_ref,
    raw_ref,
    lens_ref,
    bias_ref,
    rate_ref,
    cv_ref,
    cs_ref,
    conv_ref,
    fresh_ref,
    cols_ref,
    row_ref,
    end_ref,
    total_ref,
    prod,
    halo,
    run,
    reach,
    spread,
    near,
):
    c = pl.program_id(0)
    count = pl.num_programs(0)
    inner = vw_ref.shape[1]
    mixed = mix_ref.shape[1]
    blocks = mixed // 128
    first_row = lax.axis_index(axis) * (count * CHUNK)

    @pl.when(c == 0)
    def _():
        n = normalized(halo_ref[...], gain_ref[...].reshape(1, -1))
        halo[:, :inner] = mm(n, vw_ref[...]).astype(bf16).astype(f32)
        halo[:, inner:] = mm(n, sw_ref[...]).astype(bf16).astype(f32)
        row, g1, g2, g3, g4 = decays(first_row, raw_ref[...], lens_ref, bias_ref, rate_ref)
        row_ref[...] = row
        cols_ref[:, 0:8, :] = g1
        cols_ref[:, 8:16, :] = g2
        cols_ref[:, 16:24, :] = g3
        cols_ref[:, 24:32, :] = g4
        run[...] = jnp.zeros_like(run)
        reach[...] = jnp.zeros_like(reach)
        line = lax.broadcasted_iota(jnp.int32, spread.shape, 0) % 32
        lane = lax.broadcasted_iota(jnp.int32, spread.shape, 1)
        wanted = 12 + (lane // inner) * 8 + (lane % inner) // HEAD_DIM
        spread[...] = (line == wanted).astype(f32).astype(bf16)

        def clear(k, carry):
            near[k] = 0
            return carry

        lax.fori_loop(0, near.shape[0], clear, 0)

        def mark(k, edge):
            for shift in (-(CONV - 1), CONV - 2):
                at = (edge + shift - first_row + CHUNK) // CHUNK
                near[jnp.clip(at, 0, near.shape[0] - 1)] = 1
            return edge + lens_ref[jnp.minimum(k, PIECES - 1)]

        lax.fori_loop(0, PIECES + 1, mark, jnp.int32(0))

    taps = jnp.concatenate([cv_ref[...], cs_ref[...]], axis=1).astype(f32)
    here = slice(REACH, REACH + CHUNK)

    def put(rows, values):
        for k in range(CONV - 1):
            for b in range(blocks):
                lanes = slice(b * 128, (b + 1) * 128)
                prod[k, b, rows, :] = values[:, lanes] * taps[k : k + 1, lanes]

    put(here, mix_ref[...].astype(f32))
    ahead, behind = slice(0, REACH), slice(REACH + CHUNK, 2 * REACH + CHUNK)

    @pl.when(c == 0)
    def _():
        put(ahead, halo[HALO - REACH : HALO, :])

    @pl.when(c > 0)
    def _():
        put(ahead, before_ref[...].astype(f32)[16 - REACH :, :])

    @pl.when(c == count - 1)
    def _():
        put(behind, halo[HALO : HALO + REACH, :])

    @pl.when(c < count - 1)
    def _():
        put(behind, after_ref[...].astype(f32)[:REACH, :])

    cols = cols_ref[c]

    def convolve(masked):
        if masked:
            turned = jnp.concatenate([cols, jnp.zeros((CHUNK - 32, CHUNK), f32)], axis=0).T
            sides = [jnp.broadcast_to(turned[:, r : r + 1], (CHUNK, 128)) for r in (24, 28)]
        for b in range(blocks):
            lanes = slice(b * 128, (b + 1) * 128)
            centre = mix_ref[:, lanes].astype(f32) * taps[CONV - 1 : CONV, lanes]
            for d in range(2):
                total = centre
                for distance in range(1, CONV):
                    at = REACH + distance if d else REACH - distance
                    term = prod[CONV - 1 - distance, b, at : at + CHUNK, :]
                    if masked:
                        term = jnp.where(sides[d] >= distance, term, 0.0)
                    total = total + term
                at = d * mixed + b * 128
                conv_ref[0, 0, :, at : at + 128] = silu(total).astype(bf16)

    edges = near[c + 1]

    @pl.when(edges == 0)
    def _():
        convolve(False)

    @pl.when(edges != 0)
    def _():
        convolve(True)

    high = cols.astype(bf16).astype(f32)
    both = jnp.concatenate([high, cols - high], axis=0).astype(bf16)
    tails = mm(both, spread[...], TN)
    passing = head_lanes([cols[h : h + 1, CHUNK - 1 :] for h in range(4)])
    for d in range(2):
        x = conv_ref[0, 0, :, d * mixed : d * mixed + inner].astype(f32)
        write = conv_ref[0, 0, :, d * mixed + inner : d * mixed + inner + STATE]
        scaled = (x * tails[:, d * inner : (d + 1) * inner]).astype(bf16)
        fresh = mm(write, scaled, TN)
        fresh_ref[0, d] = fresh.astype(bf16)
        if d == 0:
            run[0] = run[0] * jnp.exp2(passing) + fresh
        else:
            run[1] = run[1] + jnp.exp2(reach[0:1, :]) * fresh
    reach[...] = reach[...] + passing

    @pl.when(c == count - 1)
    def _():
        end_ref[...] = run[...].astype(bf16)
        total_ref[...] = reach[...]


def states(axis, owners, mix, halo, gain, vw, sw, raw, lens, bias, rate, cv, cs):
    tokens, mixed = mix.shape
    chunks = tokens // CHUNK
    inner = vw.shape[1]
    rounds = chunks // owners
    per = CHUNK // 16
    last = tokens // 16 - 1
    return pl.pallas_call(
        functools.partial(states_kernel, axis),
        grid=(chunks,),
        in_specs=[
            pl.BlockSpec((CHUNK, mixed), lambda c: (c, 0)),
            pl.BlockSpec((16, mixed), lambda c: (jnp.maximum(c * per - 1, 0), 0)),
            pl.BlockSpec((16, mixed), lambda c: (jnp.minimum(c * per + per, last), 0)),
            whole(halo.shape),
            whole(gain.shape),
            whole(vw.shape),
            whole(sw.shape),
            whole(raw.shape),
            SMEM_SPEC,
            SMEM_SPEC,
            SMEM_SPEC,
            whole(cv.shape),
            whole(cs.shape),
        ],
        out_specs=[
            pl.BlockSpec((1, 1, CHUNK, 2 * mixed), lambda c: (c % rounds, c // rounds, 0, 0)),
            pl.BlockSpec((1, 2, STATE, inner), lambda c: (c, 0, 0, 0)),
            whole((chunks, 32, CHUNK)),
            whole((chunks, 8, CHUNK)),
            whole((2, STATE, inner)),
            whole((8, inner)),
        ],
        out_shape=[
            jax.ShapeDtypeStruct((rounds, owners, CHUNK, 2 * mixed), bf16),
            jax.ShapeDtypeStruct((chunks, 2, STATE, inner), bf16),
            jax.ShapeDtypeStruct((chunks, 32, CHUNK), f32),
            jax.ShapeDtypeStruct((chunks, 8, CHUNK), f32),
            jax.ShapeDtypeStruct((2, STATE, inner), bf16),
            jax.ShapeDtypeStruct((8, inner), f32),
        ],
        scratch_shapes=[
            pltpu.VMEM((CONV - 1, mixed // 128, CHUNK + 2 * REACH, 128), f32),
            pltpu.VMEM((2 * HALO, mixed), f32),
            pltpu.VMEM((2, STATE, inner), f32),
            pltpu.VMEM((8, inner), f32),
            pltpu.VMEM((64, 2 * inner), bf16),
            pltpu.SMEM((chunks + 2,), jnp.int32),
        ],
        compiler_params=params(),
        name="states",
    )(mix, mix, mix, halo, gain, vw, sw, raw, lens, bias, rate, cv, cs)


def split(x, parts):
    pieces = []
    for _ in range(parts - 1):
        pieces.append(x.astype(bf16).astype(f32))
        x = x - pieces[-1]
    return pieces + [x]


def finish_kernel(
    seq_count,
    head_count,
    end_ref,
    total_ref,
    cols_ref,
    row_ref,
    skip_ref,
    gain_ref,
    conv_hbm,
    gate_hbm,
    fresh_hbm,
    hidden_hbm,
    w_hbm,
    hop_hbm,
    out_ref,
    conv,
    gate,
    fresh,
    rest,
    weight,
    ends,
    totals,
    incoming,
    entry,
    pick,
    spread,
    inside,
    gated,
    squares,
    others,
    scales,
    sending,
    arrived,
    load,
    seq_send,
    seq_recv,
    w_send,
    w_recv,
    ss_send,
    ss_recv,
    send,
    recv,
):
    me = lax.axis_index("seq")
    head = lax.axis_index("head")
    chips = head_count // 2
    rounds, owners = conv.shape[0], conv.shape[1]
    chunks = rounds * owners
    inner = gate.shape[3]
    mixed = conv.shape[3] // 2
    rows = rounds * CHUNK
    slots = [(dy, dc) for dy in range(chips) for dc in range(2)]
    peers = [head_peer(head, chips, dy, dc) for dy, dc in slots]
    up, down, partner = peers[2], peers[2 * chips - 2], peers[1]

    def fetch(src, dst, n):
        copy = pltpu.make_async_copy(src, dst, load.at[n])
        copy.start()
        return copy

    def part(k):
        return pl.ds(k * inner, inner)

    conv_in = [fetch(conv_hbm.at[q], conv.at[q], q) for q in range(rounds)]
    fresh_in = fetch(fresh_hbm, fresh, rounds)
    gate_in = fetch(gate_hbm, gate, rounds + 1)
    mine = pl.ds(pl.multiple_of(head * rows, rows), rows)
    late = [
        fetch(hidden_hbm.at[mine, :], rest, rounds + 2),
        fetch(w_hbm, weight.at[part(0)], rounds + 3),
        fetch(hop_hbm.at[2], weight.at[part(1)], rounds + 4),
        fetch(hop_hbm.at[0], weight.at[part(2)], rounds + 5),
        fetch(hop_hbm.at[1], weight.at[part(2 * chips - 2)], rounds + 6),
    ]

    greet(
        [{"seq": (me + k) % seq_count} for k in range(1, seq_count)]
        + [{"head": p} for p in peers[1:]]
    )
    started = []

    def start(copy):
        copy.start()
        started.append(copy)
        return copy

    travelling = []
    for k in range(1, seq_count):
        target = (me + k) % seq_count
        backward = (me + k) // seq_count
        travelling.append(
            start(
                remote(
                    end_ref.at[backward], ends.at[k], seq_send.at[0, k], seq_recv.at[0, k], seq=target
                )
            )
        )
        travelling.append(
            start(remote(total_ref, totals.at[k], seq_send.at[1, k], seq_recv.at[1, k], seq=target))
        )
    half = inner // 2
    far = 4 * inner
    top, bottom = pl.ds(0, half), pl.ds(half, half)
    t1 = start(
        remote(
            hop_hbm.at[0, top], weight.at[pl.ds(far, half)], w_send.at[0], w_recv.at[0], head=up
        )
    )
    t3 = start(
        remote(
            hop_hbm.at[1, bottom],
            weight.at[pl.ds(far + half, half)],
            w_send.at[1],
            w_recv.at[1],
            head=down,
        )
    )
    t2 = start(remote(hop_hbm.at[0], weight.at[part(3)], w_send.at[2], w_recv.at[2], head=partner))
    t4 = start(
        remote(hop_hbm.at[1], weight.at[part(2 * chips - 1)], w_send.at[3], w_recv.at[3], head=partner)
    )

    i = lax.broadcasted_iota(jnp.int32, (CHUNK, CHUNK), 0)
    j = lax.broadcasted_iota(jnp.int32, (CHUNK, CHUNK), 1)
    lower = i >= j
    upper = i <= j
    low = j < HEAD_DIM
    skip = head_lanes([jnp.full((1, 1), skip_ref[h], f32) for h in range(4)])
    sub = lax.broadcasted_iota(jnp.int32, (8, CHUNK), 0)
    line = lax.broadcasted_iota(jnp.int32, pick.shape[1:], 0)
    block = lax.broadcasted_iota(jnp.int32, pick.shape[1:], 1) // CHUNK
    sign = jnp.where(block < 4, 1.0, -1.0)
    chosen = jnp.where((line < 24) & (line % 8 == block), sign, 0.0).astype(bf16)
    for u in range(pick.shape[0]):
        pick[u] = chosen
    line = lax.broadcasted_iota(jnp.int32, spread.shape, 0)
    lane = lax.broadcasted_iota(jnp.int32, spread.shape, 1)
    wanted = (lane // inner) * 8 + (lane % inner) // HEAD_DIM
    spread[...] = (line % 16 == wanted).astype(f32).astype(bf16)

    def within(q, d, u):
        c = d * rounds + q
        row = row_ref[c]
        lines = jnp.concatenate(split(jnp.where(sub < 4, -row, row), 3), axis=0)
        for n in range(8):
            own = lax.broadcasted_iota(jnp.int32, lines.shape, 0) % 8 == n
            pick[u, 32:56, n * CHUNK : (n + 1) * CHUNK] = jnp.where(own, lines, 0.0).astype(bf16)
        left = jnp.concatenate(
            split(cols_ref[c, 0:8, :], 3)
            + [jnp.zeros((8, CHUNK), f32), jnp.ones((24, CHUNK), f32), jnp.zeros((8, CHUNK), f32)],
            axis=0,
        ).astype(bf16)
        made = mm(left, pick[u], TN)
        pair = []
        for e, keep in ((0, lower), (1, upper)):
            base = e * mixed + inner
            write = conv[q, d, :, base : base + STATE]
            read = conv[q, d, :, base + STATE : base + 2 * STATE]
            pair.append(jnp.where(keep, mm(read, write, NT), 0.0))
        for p in range(2):
            weights = ([], [])
            for h in (2 * p, 2 * p + 1):
                table = jnp.exp2(
                    jnp.where(
                        lower,
                        made[:, h * CHUNK : (h + 1) * CHUNK],
                        made[:, (4 + h) * CHUNK : (5 + h) * CHUNK],
                    )
                )
                for e in range(2):
                    weights[e].append((pair[e] * table).astype(bf16))
            for e in range(2):
                at = e * mixed + p * CHUNK
                x = conv[q, d, :, at : at + CHUNK]
                zero = jnp.zeros_like(x)
                stacked = jnp.concatenate([jnp.where(low, x, zero), jnp.where(low, zero, x)], axis=0)
                made_here = mm(jnp.concatenate(weights[e], axis=1), stacked)
                made_here = made_here + skip[:, p * CHUNK : (p + 1) * CHUNK] * x.astype(f32)
                inside[q, d, :, e * inner + p * CHUNK : e * inner + (p + 1) * CHUNK] = made_here

    for q in range(rounds):
        conv_in[q].wait()

        def step(n, carry, q=q):
            for u in range(2):
                within(q, 2 * n + u, u)
            return carry

        lax.fori_loop(0, owners // 2, step, 0)

    for copy in travelling:
        copy.wait_recv()
    t1.wait_recv()
    t3.wait_recv()
    t5 = start(
        remote(weight.at[part(4)], weight.at[part(5)], w_send.at[4], w_recv.at[4], head=partner)
    )
    incoming[...] = jnp.zeros_like(incoming)
    for k in range(seq_count - 1, 0, -1):

        @pl.when(k <= me)
        def _(k=k):
            incoming[0] = incoming[0] * jnp.exp2(totals[k, 0:1, :]) + ends[k].astype(f32)

    for k in range(1, seq_count):

        @pl.when(k > me)
        def _(k=k):
            incoming[1] = incoming[1] * jnp.exp2(totals[k, 0:1, :]) + ends[k].astype(f32)

    fresh_in.wait()

    def passing(c):
        return jnp.exp2(head_lanes([cols_ref[c, h : h + 1, CHUNK - 1 :] for h in range(4)]))

    def walk(c, carry):
        b = chunks - 1 - c
        for e, at in ((0, c), (1, b)):
            state = incoming[e]
            entry[e, at] = state.astype(bf16)
            incoming[e] = state * passing(at) + fresh[at, e].astype(f32)
        return carry

    lax.fori_loop(0, chunks, walk, 0)
    gate_in.wait()

    ones = jnp.ones((8, inner), bf16)
    gain = gain_ref[...].reshape(1, -1).astype(f32)
    sixteen = lax.broadcasted_iota(jnp.int32, (2 * owners, CHUNK), 0)

    def carried(q, d, sums):
        c = d * rounds + q
        left = jnp.concatenate(split(cols_ref[c, 8:24, :], 2), axis=0).astype(bf16)
        scale = mm(left, spread[...], TN)
        act = silu(gate[q, d].astype(f32))
        for e in range(2):
            at = e * mixed + inner + STATE
            lanes = slice(e * inner, (e + 1) * inner)
            part_in = mm(conv[q, d, :, at : at + STATE], entry[e, c])
            value = (inside[q, d, :, lanes] + part_in * scale[:, lanes]) * act
            gated[q, d, :, lanes] = value.astype(bf16)
            square = mm(ones, (value * value).astype(bf16), NT)
            square = jnp.concatenate([square] * (2 * owners // 8), axis=0)
            sums = jnp.where(sixteen == 2 * d + e, square, sums)
        return sums

    def combine(q):
        for k in range(1, head_count):
            ss[q][k - 1].wait_recv()
        total = squares[q]
        for k in range(1, head_count):
            total = total + others[q, k]
        total = lax.rsqrt(total * (1.0 / (inner * head_count)) + epsilon)
        for d in range(owners):
            scales[q, d, 0:2, :] = total[2 * d : 2 * d + 2, :]
        for k in range(head_count):
            d = peers[k]
            scale = jnp.concatenate(
                [scales[q, d, 0:2, :], jnp.zeros((CHUNK - 2, CHUNK), f32)], axis=0
            ).T
            both = gated[q, d, :, :inner].astype(f32) * scale[:, 0:1]
            both = both + gated[q, d, :, inner:].astype(f32) * scale[:, 1:2]
            both = (both * gain).astype(bf16)
            if k == 0:
                arrived[q * CHUNK : (q + 1) * CHUNK, 0:inner] = both
            else:
                sending[q, k] = both
        return [
            start(
                remote(
                    sending.at[q, k],
                    arrived.at[pl.ds(q * CHUNK, CHUNK), part(k)],
                    send.at[q, k],
                    recv.at[q, k],
                    head=peers[k],
                )
            )
            for k in sorted(range(1, head_count), key=lambda k: -min(slots[k][0], chips - slots[k][0]))
        ]

    ss, pieces = [], []
    for q in range(rounds):
        squares[q] = lax.fori_loop(
            0, owners, lambda d, sums, q=q: carried(q, d, sums), jnp.zeros((2 * owners, CHUNK), f32)
        )
        ss.append(
            [
                start(
                    remote(
                        squares.at[q], others.at[q, k], ss_send.at[q, k], ss_recv.at[q, k], head=peers[k]
                    )
                )
                for k in range(1, head_count)
            ]
        )
        if q:
            pieces.append(combine(q - 1))
    pieces.append(combine(rounds - 1))

    for copy in late:
        copy.wait()
    for copy in (t2, t4, t5):
        copy.wait_recv()
    width = out_ref.shape[1]
    step_lanes = 256
    early = (rounds - 1) * CHUNK
    for first, count, done in ((0, early, pieces[:-1]), (early, CHUNK, pieces[-1:])):
        for batch in done:
            for copy in batch:
                copy.wait_recv()
        if count:

            def project_out(b, carry, first=first, count=count):
                lanes = pl.ds(pl.multiple_of(b * step_lanes, step_lanes), step_lanes)
                here = pl.ds(first, count)
                out_ref[here, lanes] = (
                    mm(arrived[here, :], weight[:, lanes]) + rest[here, lanes].astype(f32)
                ).astype(bf16)
                return carry

            lax.fori_loop(0, width // step_lanes, project_out, 0)
    for copy in started:
        copy.wait_send()


def finish(mesh_shape, end, total, cols, row, skip, gain, conv, gate, fresh, hidden, w, hop):
    seq_count, head_count = mesh_shape
    rounds, owners = conv.shape[:2]
    rows = rounds * CHUNK
    inner = gate.shape[3]
    width = hidden.shape[1]
    dma = pltpu.SemaphoreType.DMA
    return pl.pallas_call(
        functools.partial(finish_kernel, seq_count, head_count),
        in_specs=[
            whole(end.shape),
            whole(total.shape),
            whole(cols.shape),
            whole(row.shape),
            SMEM_SPEC,
            whole(gain.shape),
        ]
        + [ANY_SPEC] * 6,
        out_specs=whole((rows, width)),
        out_shape=jax.ShapeDtypeStruct((rows, width), bf16),
        scratch_shapes=[
            pltpu.VMEM(conv.shape, bf16),
            pltpu.VMEM(gate.shape, bf16),
            pltpu.VMEM(fresh.shape, bf16),
            pltpu.VMEM((rows, width), bf16),
            pltpu.VMEM((head_count * inner, width), bf16),
            pltpu.VMEM((seq_count,) + end.shape[1:], bf16),
            pltpu.VMEM((seq_count,) + total.shape, f32),
            pltpu.VMEM(end.shape, f32),
            pltpu.VMEM((2, rounds * owners) + end.shape[1:], bf16),
            pltpu.VMEM((2, 64, 8 * CHUNK), bf16),
            pltpu.VMEM((32, 2 * inner), bf16),
            pltpu.VMEM((rounds, owners, CHUNK, 2 * inner), f32),
            pltpu.VMEM((rounds, owners, CHUNK, 2 * inner), bf16),
            pltpu.VMEM((rounds, 2 * owners, CHUNK), f32),
            pltpu.VMEM((rounds, head_count, 2 * owners, CHUNK), f32),
            pltpu.VMEM((rounds, owners, 8, CHUNK), f32),
            pltpu.VMEM((rounds, head_count, CHUNK, inner), bf16),
            pltpu.VMEM((rows, head_count * inner), bf16),
            dma((rounds + 7,)),
            dma((2, seq_count)),
            dma((2, seq_count)),
            dma((5,)),
            dma((5,)),
            dma((rounds, head_count)),
            dma((rounds, head_count)),
            dma((rounds, head_count)),
            dma((rounds, head_count)),
        ],
        compiler_params=params(collective_id=1, has_side_effects=True),
        name="finish",
    )(end, total, cols, row, skip, gain, conv, gate, fresh, hidden, w, hop)


def local(
    hidden_in,
    norm_gain,
    gate_weight,
    value_weight,
    state_weight,
    step_weight,
    step_bias,
    decay_log,
    skip_gain,
    conv_value,
    conv_state,
    output_gain,
    output_weight,
    piece_lengths,
):
    seq_count, head_count = lax.axis_size("seq"), lax.axis_size("head")
    shape = (seq_count, head_count)
    gate, mix, raw, halo, hop = project(
        shape, hidden_in, norm_gain, gate_weight, value_weight, state_weight, step_weight, output_weight
    )
    conv, fresh, cols, row, end, total = states(
        "seq",
        head_count,
        mix,
        halo,
        norm_gain,
        value_weight,
        state_weight,
        raw,
        piece_lengths,
        step_bias,
        decay_log,
        conv_value,
        conv_state,
    )
    return finish(
        shape,
        end,
        total,
        cols,
        row,
        skip_gain,
        output_gain,
        conv,
        gate,
        fresh,
        hidden_in,
        output_weight,
        hop,
    )


def solution(mesh):
    in_specs = (
        P("seq", None),
        P(),
        P(None, "head"),
        P(None, "head"),
        P(),
        P(None, "head"),
        P("head"),
        P("head"),
        P("head"),
        P(None, "head"),
        P(),
        P("head"),
        P("head", None),
        P(),
    )
    out_specs = P(("seq", "head"), None)
    return jax.shard_map(local, mesh=mesh, in_specs=in_specs, out_specs=out_specs, check_vma=False)
```

time: 152 us -> 124 us (0.82)
  Pallas kernels: 147 us -> 119 us
    pallas_call x3 -> x1, Pallas kernels: 91.1 us -> 63 us  [finish(): pl.pallas_call(functools.partial(finish_kernel, seq_count, head_count), i...]
where the time goes in v2:
time: 124 us; the launch traced here: 123 us
  Pallas kernels  119 us (96%)
  local copies, waits for them, and re-layouts  3.84 us (3%)
    pallas_call x1, Pallas kernels, finish(): pl.pallas_call(functools.partial(finish_kernel, seq_count, head_count), i...  63 us
    pallas_call x1, Pallas kernels, states(): pl.pallas_call(functools.partial(states_kernel, axis), grid=(chunks,), in...  32 us
    pallas_call x1, Pallas kernels, project(): pl.pallas_call(functools.partial(project_kernel, mesh_shape), grid=(token...  23.9 us
    unnamed x2, local copies, waits for them, and re-layouts  3.84 us

profile of v2, /device:TPU:1, one launch (start us, length us, event | category | flops | bytes accessed | tf_op | source)
XLA Modules:
  0.0 122.8 jit_solution(16437001869463239424)
XLA Ops:
  0.0 1.6 %copy.15.tw_ref = bf16[1024,4]{1,0:T(8,128)(2,1)} copy(bf16[1024,4]{0,1:T(4,128)(2,1)} %param.19) | data formatting | bytes 16384 | tf_op args[5]
  1.6 23.9 %project.1 = (bf16[4,8,128,256]{3,2,1,0:T(8,128)(2,1)}, bf16[4096,512]{1,0:T(8,128)(2,1)}, f32[32,8,128]{2,1,0:T(8,128)}, bf16[32,1024]{1,0:T(8,128)(2,1)}, bf16[3,256,1024]{2,1,0:T(8,128)(2,1)}) custom-call(bf16[4096,1024]{1,0:T(8,128)(2,1)} %hidden_hbm.1, bf16[1024]{0:T(1024)(128)(2,1)} %gain_ref.4, bf16[1024,256]{1,0:T(8,128)(2,1)} %gw_ref.1, ...), custom_call_target="tpu_custom_call" | custom-call | tf_op jit(solution)/shard_map/project/pallas_call | solution.py:165
  25.5 32.0 %states.1 = (bf16[4,8,128,1024]{3,2,1,0:T(8,128)(2,1)}, bf16[32,2,128,256]{3,2,1,0:T(8,128)(2,1)}, f32[32,32,128]{2,1,0:T(8,128)}, f32[32,8,128]{2,1,0:T(8,128)}...) custom-call(bf16[4096,512]{1,0:T(8,128)(2,1)} %get-tuple-element.16.mix_ref.before_ref.after_ref, ...), custom_call_target="tpu_custom_call" | custom-call | tf_op jit(solution)/shard_map/states/pallas_call | solution.py:412
  57.5 63.0 %finish.1 = bf16[512,1024]{1,0:T(8,128)(2,1)} custom-call(bf16[2,128,256]{2,1,0:T(8,128)(2,1)} %get-tuple-element.19.end_ref, f32[8,256]{1,0:T(8,128)} %get-tuple-element.20.total_ref, f32[32,32,128]{2,1,0:T(8,128)} %get-tuple-element.21.cols_ref, f32[32,8,128]{2,1,0:T(8,128)} %get-tuple-element.22.row_ref, f32[4]{0:T(128)} %skip_ref.1, ...), custom_call_target="tpu_custom_call" | custom-call | tf_op jit(solution)/shard_map/finish/pallas_call | solution.py:800
  120.5 2.3 %copy.17 = bf16[512,1024]{1,0:T(8,128)(2,1)} copy(bf16[512,1024]{1,0:T(8,128)(2,1)} %finish.1) | data formatting | bytes 2097152

commit v3 on v2

--- a/solution.py
+++ b/solution.py
@@ -87,14 +87,16 @@
     before = (me + seq_count - 1) % seq_count
     first, last = pl.ds(0, HALO), pl.ds(tokens - HALO, HALO)
     low, high = pl.ds(0, HALO), pl.ds(HALO, HALO)
+    half = w.shape[0] // 2
+    top, bottom = pl.ds(0, half), pl.ds(half, half)
     up = head_peer(head, chips, 1, 0)
     down = head_peer(head, chips, chips - 1, 0)
     partner = head_peer(head, chips, 0, 1)
     return (
         remote(hidden.at[last], halo.at[low], send.at[0], recv.at[0], seq=after),
         remote(hidden.at[first], halo.at[high], send.at[1], recv.at[1], seq=before),
-        remote(w, hop.at[0], send.at[2], recv.at[2], head=up),
-        remote(w, hop.at[1], send.at[3], recv.at[3], head=down),
+        remote(w.at[top], hop.at[0, top], send.at[2], recv.at[2], head=up),
+        remote(w.at[bottom], hop.at[1, bottom], send.at[3], recv.at[3], head=down),
         remote(w, hop.at[2], send.at[4], recv.at[4], head=partner),
     ), [{"seq": after}, {"seq": before}, {"head": up}, {"head": down}, {"head": partner}]
 
@@ -115,6 +117,7 @@
     halo,
     hop,
     turned,
+    rows,
     send,
     recv,
 ):
@@ -127,11 +130,7 @@
         for where in peers:
             pl.semaphore_signal(barrier, inc=1, device_id=where, device_id_type=MESH)
         narrow = tw_ref[...].astype(f32)
-        depth, few = narrow.shape
-        padded = jnp.concatenate(
-            [narrow, narrow, jnp.zeros((depth, CHUNK - 2 * few), f32)], axis=1
-        )
-        turned[...] = padded.T[:8].astype(bf16)
+        turned[...] = jnp.concatenate([narrow, narrow], axis=0).astype(bf16)
 
     @pl.when(i == 1)
     def _():
@@ -140,15 +139,18 @@
             copy.start()
 
     inner = vw_ref.shape[1]
-    n = normalized(h_ref[...], gain_ref[...].reshape(1, -1))
-    gate = mm(n, gw_ref[...]).astype(bf16)
+    gain = gain_ref[...].reshape(1, -1)
     for q in range(gate_ref.shape[0]):
-        gate_ref[q, 0] = gate[q * CHUNK : (q + 1) * CHUNK]
-    mix_ref[:, :inner] = mm(n, vw_ref[...]).astype(bf16)
-    mix_ref[:, inner:] = mm(n, sw_ref[...]).astype(bf16)
-    raw = mm(turned[...], n, NT)
-    for q in range(raw.shape[1] // CHUNK):
-        raw_ref[q] = raw[:, q * CHUNK : (q + 1) * CHUNK]
+        at = slice(q * CHUNK, (q + 1) * CHUNK)
+        for r in range(0, CHUNK, 32):
+            rows[q * CHUNK + r : q * CHUNK + r + 32, :] = normalized(
+                h_ref[q * CHUNK + r : q * CHUNK + r + 32, :], gain
+            )
+        n = rows[at, :]
+        gate_ref[q, 0] = mm(n, gw_ref[...]).astype(bf16)
+        mix_ref[at, :inner] = mm(n, vw_ref[...]).astype(bf16)
+        mix_ref[at, inner:] = mm(n, sw_ref[...]).astype(bf16)
+        raw_ref[q] = mm(turned[...], n, NT)
 
     @pl.when(i == pl.num_programs(0) - 1)
     def _():
@@ -191,6 +193,7 @@
         ],
         scratch_shapes=[
             pltpu.VMEM((8, width), bf16),
+            pltpu.VMEM((rows, width), bf16),
             pltpu.SemaphoreType.DMA((5,)),
             pltpu.SemaphoreType.DMA((5,)),
         ],
@@ -283,14 +286,15 @@
     spread,
     near,
 ):
-    c = pl.program_id(0)
-    count = pl.num_programs(0)
+    g = pl.program_id(0)
+    groups = pl.num_programs(0)
     inner = vw_ref.shape[1]
-    mixed = mix_ref.shape[1]
+    rows, mixed = mix_ref.shape
+    rounds = rows // CHUNK
     blocks = mixed // 128
-    first_row = lax.axis_index(axis) * (count * CHUNK)
-
-    @pl.when(c == 0)
+    first_row = lax.axis_index(axis) * (groups * rows)
+
+    @pl.when(g == 0)
     def _():
         n = normalized(halo_ref[...], gain_ref[...].reshape(1, -1))
         halo[:, :inner] = mm(n, vw_ref[...]).astype(bf16).astype(f32)
@@ -316,87 +320,80 @@
 
         def mark(k, edge):
             for shift in (-(CONV - 1), CONV - 2):
-                at = (edge + shift - first_row + CHUNK) // CHUNK
+                at = (edge + shift - first_row + rows) // rows
                 near[jnp.clip(at, 0, near.shape[0] - 1)] = 1
             return edge + lens_ref[jnp.minimum(k, PIECES - 1)]
 
         lax.fori_loop(0, PIECES + 1, mark, jnp.int32(0))
 
-    taps = jnp.concatenate([cv_ref[...], cs_ref[...]], axis=1).astype(f32)
-    here = slice(REACH, REACH + CHUNK)
-
-    def put(rows, values):
+    taps = jnp.concatenate([cv_ref[...], cs_ref[...]], axis=1).astype(f32) * 0.5
+
+    def put(b, at, values):
+        lanes = slice(b * 128, (b + 1) * 128)
         for k in range(CONV - 1):
-            for b in range(blocks):
-                lanes = slice(b * 128, (b + 1) * 128)
-                prod[k, b, rows, :] = values[:, lanes] * taps[k : k + 1, lanes]
-
-    put(here, mix_ref[...].astype(f32))
-    ahead, behind = slice(0, REACH), slice(REACH + CHUNK, 2 * REACH + CHUNK)
-
-    @pl.when(c == 0)
-    def _():
-        put(ahead, halo[HALO - REACH : HALO, :])
-
-    @pl.when(c > 0)
-    def _():
-        put(ahead, before_ref[...].astype(f32)[16 - REACH :, :])
-
-    @pl.when(c == count - 1)
-    def _():
-        put(behind, halo[HALO : HALO + REACH, :])
-
-    @pl.when(c < count - 1)
-    def _():
-        put(behind, after_ref[...].astype(f32)[:REACH, :])
-
-    cols = cols_ref[c]
-
-    def convolve(masked):
+            prod[k, b, at : at + values.shape[0], :] = values * taps[k : k + 1, lanes]
+
+    def group(masked):
+        for b in range(blocks):
+            lanes = slice(b * 128, (b + 1) * 128)
+            ahead = before_ref[:, lanes].astype(f32)[16 - REACH :, :]
+            put(b, 0, jnp.where(g == 0, halo[HALO - REACH : HALO, lanes], ahead))
+            behind = after_ref[:, lanes].astype(f32)[:REACH, :]
+            put(b, REACH + rows, jnp.where(g == groups - 1, halo[HALO : HALO + REACH, lanes], behind))
+            for q in range(rounds):
+                put(b, REACH + q * CHUNK, mix_ref[q * CHUNK : (q + 1) * CHUNK, lanes].astype(f32))
+        for q in range(rounds):
+            chunk(q, masked)
+
+    def chunk(q, masked):
+        cols = cols_ref[g * rounds + q]
+        high = cols.astype(bf16).astype(f32)
+        both = jnp.concatenate([high, cols - high], axis=0).astype(bf16)
+        tails = mm(both, spread[...], TN)
+        passing = head_lanes([cols[h : h + 1, CHUNK - 1 :] for h in range(4)])
         if masked:
             turned = jnp.concatenate([cols, jnp.zeros((CHUNK - 32, CHUNK), f32)], axis=0).T
             sides = [jnp.broadcast_to(turned[:, r : r + 1], (CHUNK, 128)) for r in (24, 28)]
-        for b in range(blocks):
+        write = [None, None]
+        for b in [inner // 128] + list(range(inner // 128)) + list(range(inner // 128 + 1, blocks)):
             lanes = slice(b * 128, (b + 1) * 128)
-            centre = mix_ref[:, lanes].astype(f32) * taps[CONV - 1 : CONV, lanes]
+            centre = mix_ref[q * CHUNK : (q + 1) * CHUNK, lanes].astype(f32) * taps[CONV - 1 : CONV, lanes]
             for d in range(2):
-                total = centre
+                half = centre
                 for distance in range(1, CONV):
-                    at = REACH + distance if d else REACH - distance
+                    at = REACH + q * CHUNK + (distance if d else -distance)
                     term = prod[CONV - 1 - distance, b, at : at + CHUNK, :]
                     if masked:
                         term = jnp.where(sides[d] >= distance, term, 0.0)
-                    total = total + term
+                    half = half + term
+                value = half * jnp.tanh(half) + half
                 at = d * mixed + b * 128
-                conv_ref[0, 0, :, at : at + 128] = silu(total).astype(bf16)
-
-    edges = near[c + 1]
+                narrow = value.astype(bf16)
+                conv_ref[q, 0, :, at : at + 128] = narrow
+                if b == inner // 128:
+                    write[d] = narrow
+                elif b < inner // 128:
+                    at = d * inner + b * 128
+                    scaled = (value * tails[:, at : at + 128]).astype(bf16)
+                    fresh = mm(write[d], scaled, TN)
+                    fresh_ref[q, d, :, lanes] = fresh.astype(bf16)
+                    if d == 0:
+                        run[0, :, lanes] = run[0, :, lanes] * jnp.exp2(passing[:, lanes]) + fresh
+                    else:
+                        run[1, :, lanes] = run[1, :, lanes] + jnp.exp2(reach[0:1, lanes]) * fresh
+        reach[...] = reach[...] + passing
+
+    edges = near[g + 1]
 
     @pl.when(edges == 0)
     def _():
-        convolve(False)
+        group(False)
 
     @pl.when(edges != 0)
     def _():
-        convolve(True)
-
-    high = cols.astype(bf16).astype(f32)
-    both = jnp.concatenate([high, cols - high], axis=0).astype(bf16)
-    tails = mm(both, spread[...], TN)
-    passing = head_lanes([cols[h : h + 1, CHUNK - 1 :] for h in range(4)])
-    for d in range(2):
-        x = conv_ref[0, 0, :, d * mixed : d * mixed + inner].astype(f32)
-        write = conv_ref[0, 0, :, d * mixed + inner : d * mixed + inner + STATE]
-        scaled = (x * tails[:, d * inner : (d + 1) * inner]).astype(bf16)
-        fresh = mm(write, scaled, TN)
-        fresh_ref[0, d] = fresh.astype(bf16)
-        if d == 0:
-            run[0] = run[0] * jnp.exp2(passing) + fresh
-        else:
-            run[1] = run[1] + jnp.exp2(reach[0:1, :]) * fresh
-    reach[...] = reach[...] + passing
-
-    @pl.when(c == count - 1)
+        group(True)
+
+    @pl.when(g == groups - 1)
     def _():
         end_ref[...] = run[...].astype(bf16)
         total_ref[...] = reach[...]
@@ -407,13 +404,14 @@
     chunks = tokens // CHUNK
     inner = vw.shape[1]
     rounds = chunks // owners
-    per = CHUNK // 16
+    rows = rounds * CHUNK
+    per = rows // 16
     last = tokens // 16 - 1
     return pl.pallas_call(
         functools.partial(states_kernel, axis),
-        grid=(chunks,),
+        grid=(owners,),
         in_specs=[
-            pl.BlockSpec((CHUNK, mixed), lambda c: (c, 0)),
+            pl.BlockSpec((rows, mixed), lambda c: (c, 0)),
             pl.BlockSpec((16, mixed), lambda c: (jnp.maximum(c * per - 1, 0), 0)),
             pl.BlockSpec((16, mixed), lambda c: (jnp.minimum(c * per + per, last), 0)),
             whole(halo.shape),
@@ -428,8 +426,8 @@
             whole(cs.shape),
         ],
         out_specs=[
-            pl.BlockSpec((1, 1, CHUNK, 2 * mixed), lambda c: (c % rounds, c // rounds, 0, 0)),
-            pl.BlockSpec((1, 2, STATE, inner), lambda c: (c, 0, 0, 0)),
+            pl.BlockSpec((rounds, 1, CHUNK, 2 * mixed), lambda c: (0, c, 0, 0)),
+            pl.BlockSpec((rounds, 2, STATE, inner), lambda c: (c, 0, 0, 0)),
             whole((chunks, 32, CHUNK)),
             whole((chunks, 8, CHUNK)),
             whole((2, STATE, inner)),
@@ -444,12 +442,12 @@
             jax.ShapeDtypeStruct((8, inner), f32),
         ],
         scratch_shapes=[
-            pltpu.VMEM((CONV - 1, mixed // 128, CHUNK + 2 * REACH, 128), f32),
+            pltpu.VMEM((CONV - 1, mixed // 128, rows + 2 * REACH, 128), f32),
             pltpu.VMEM((2 * HALO, mixed), f32),
             pltpu.VMEM((2, STATE, inner), f32),
             pltpu.VMEM((8, inner), f32),
             pltpu.VMEM((64, 2 * inner), bf16),
-            pltpu.SMEM((chunks + 2,), jnp.int32),
+            pltpu.SMEM((owners + 2,), jnp.int32),
         ],
         compiler_params=params(),
         name="states",
@@ -532,12 +530,16 @@
     fresh_in = fetch(fresh_hbm, fresh, rounds)
     gate_in = fetch(gate_hbm, gate, rounds + 1)
     mine = pl.ds(pl.multiple_of(head * rows, rows), rows)
+    half = inner // 2
+    side = (2 * chips - 2) * inner
+    far = 4 * inner
+    top, bottom = pl.ds(0, half), pl.ds(half, half)
     late = [
         fetch(hidden_hbm.at[mine, :], rest, rounds + 2),
         fetch(w_hbm, weight.at[part(0)], rounds + 3),
         fetch(hop_hbm.at[2], weight.at[part(1)], rounds + 4),
-        fetch(hop_hbm.at[0], weight.at[part(2)], rounds + 5),
-        fetch(hop_hbm.at[1], weight.at[part(2 * chips - 2)], rounds + 6),
+        fetch(hop_hbm.at[0, top], weight.at[pl.ds(2 * inner, half)], rounds + 5),
+        fetch(hop_hbm.at[1, bottom], weight.at[pl.ds(side + half, half)], rounds + 6),
     ]
 
     greet(
@@ -565,27 +567,18 @@
         travelling.append(
             start(remote(total_ref, totals.at[k], seq_send.at[1, k], seq_recv.at[1, k], seq=target))
         )
-    half = inner // 2
-    far = 4 * inner
-    top, bottom = pl.ds(0, half), pl.ds(half, half)
-    t1 = start(
-        remote(
-            hop_hbm.at[0, top], weight.at[pl.ds(far, half)], w_send.at[0], w_recv.at[0], head=up
-        )
-    )
-    t3 = start(
-        remote(
-            hop_hbm.at[1, bottom],
-            weight.at[pl.ds(far + half, half)],
-            w_send.at[1],
-            w_recv.at[1],
-            head=down,
-        )
-    )
-    t2 = start(remote(hop_hbm.at[0], weight.at[part(3)], w_send.at[2], w_recv.at[2], head=partner))
-    t4 = start(
-        remote(hop_hbm.at[1], weight.at[part(2 * chips - 1)], w_send.at[3], w_recv.at[3], head=partner)
-    )
+    def weigh(n, src, row, where, count=half):
+        at = weight.at[pl.ds(row, count)]
+        return start(remote(src, at, w_send.at[n], w_recv.at[n], head=where))
+
+    u1 = weigh(0, w_hbm.at[bottom], 2 * inner + half, up)
+    u2 = weigh(1, w_hbm.at[top], side, down)
+    t1 = weigh(2, hop_hbm.at[0, top], far, up)
+    t3 = weigh(3, hop_hbm.at[1, bottom], far + half, down)
+    beside = [
+        weigh(4, hop_hbm.at[0, top], 3 * inner, partner),
+        weigh(5, hop_hbm.at[1, bottom], side + inner + half, partner),
+    ]
 
     i = lax.broadcasted_iota(jnp.int32, (CHUNK, CHUNK), 0)
     j = lax.broadcasted_iota(jnp.int32, (CHUNK, CHUNK), 1)
@@ -657,11 +650,13 @@
 
     for copy in travelling:
         copy.wait_recv()
-    t1.wait_recv()
-    t3.wait_recv()
-    t5 = start(
-        remote(weight.at[part(4)], weight.at[part(5)], w_send.at[4], w_recv.at[4], head=partner)
-    )
+    for copy in (u1, u2, t1, t3):
+        copy.wait_recv()
+    beside += [
+        weigh(6, weight.at[pl.ds(2 * inner + half, half)], 3 * inner + half, partner),
+        weigh(7, weight.at[pl.ds(side, half)], side + inner, partner),
+        weigh(8, weight.at[part(4)], 5 * inner, partner, inner),
+    ]
     incoming[...] = jnp.zeros_like(incoming)
     for k in range(seq_count - 1, 0, -1):
 
@@ -766,7 +761,7 @@
 
     for copy in late:
         copy.wait()
-    for copy in (t2, t4, t5):
+    for copy in beside:
         copy.wait_recv()
     width = out_ref.shape[1]
     step_lanes = 256
@@ -832,8 +827,8 @@
             dma((rounds + 7,)),
             dma((2, seq_count)),
             dma((2, seq_count)),
-            dma((5,)),
-            dma((5,)),
+            dma((9,)),
+            dma((9,)),
             dma((rounds, head_count)),
             dma((rounds, head_count)),
             dma((rounds, head_count)),
@@ -863,7 +858,7 @@
     seq_count, head_count = lax.axis_size("seq"), lax.axis_size("head")
     shape = (seq_count, head_count)
     gate, mix, raw, halo, hop = project(
-        shape, hidden_in, norm_gain, gate_weight, value_weight, state_weight, step_weight, output_weight
+        shape, hidden_in, norm_gain, gate_weight, value_weight, state_weight, step_weight.T, output_weight
     )
     conv, fresh, cols, row, end, total = states(
         "seq",

time: 124 us -> 105 us (0.85)
  Pallas kernels: 119 us -> 101 us
  local copies, waits for them, and re-layouts: 3.84 us -> 2.26 us
    pallas_call x1, Pallas kernels: 32 us -> 17.8 us  [states(): pl.pallas_call(functools.partial(states_kernel, axis), grid=(owners,), in...]
    pallas_call x1, Pallas kernels: 23.9 us -> 19.6 us  [project(): pl.pallas_call(functools.partial(project_kernel, mesh_shape), grid=(token...]
    unnamed x2 -> x1, local copies, waits for them, and re-layouts: 3.84 us -> 2.26 us
where the time goes in v3:
time: 105 us; the launch traced here: 103 us
  Pallas kernels  101 us (96%)
  local copies, waits for them, and re-layouts  2.26 us (2%)
    pallas_call x1, Pallas kernels, finish(): pl.pallas_call(functools.partial(finish_kernel, seq_count, head_count), i...  63.7 us
    pallas_call x1, Pallas kernels, project(): pl.pallas_call(functools.partial(project_kernel, mesh_shape), grid=(token...  19.6 us
    pallas_call x1, Pallas kernels, states(): pl.pallas_call(functools.partial(states_kernel, axis), grid=(owners,), in...  17.8 us
    unnamed x1, local copies, waits for them, and re-layouts  2.26 us

profile of v3, /device:TPU:1, one launch (start us, length us, event | category | flops | bytes accessed | tf_op | source)
XLA Modules:
  0.0 103.4 jit_solution(15691380287679639474)
XLA Ops:
  0.0 19.6 %project.1 = (bf16[4,8,128,256]{3,2,1,0:T(8,128)(2,1)}, bf16[4096,512]{1,0:T(8,128)(2,1)}, f32[32,8,128]{2,1,0:T(8,128)}, bf16[32,1024]{1,0:T(8,128)(2,1)}, bf16[3,256,1024]{2,1,0:T(8,128)(2,1)}) custom-call(bf16[4096,1024]{1,0:T(8,128)(2,1)} %hidden_hbm.1, bf16[1024]{0:T(1024)(128)(2,1)} %gain_ref.4, bf16[1024,256]{1,0:T(8,128)(2,1)} %gw_ref.1, ...), custom_call_target="tpu_custom_call" | custom-call | tf_op jit(solution)/shard_map/project/pallas_call | solution.py:167
  19.6 17.8 %states.1 = (bf16[4,8,128,1024]{3,2,1,0:T(8,128)(2,1)}, bf16[32,2,128,256]{3,2,1,0:T(8,128)(2,1)}, f32[32,32,128]{2,1,0:T(8,128)}, f32[32,8,128]{2,1,0:T(8,128)}...) custom-call(bf16[4096,512]{1,0:T(8,128)(2,1)} %get-tuple-element.16.mix_ref.before_ref.after_ref, ...), custom_call_target="tpu_custom_call" | custom-call | tf_op jit(solution)/shard_map/states/pallas_call | solution.py:410
  37.4 63.7 %finish.1 = bf16[512,1024]{1,0:T(8,128)(2,1)} custom-call(bf16[2,128,256]{2,1,0:T(8,128)(2,1)} %get-tuple-element.19.end_ref, f32[8,256]{1,0:T(8,128)} %get-tuple-element.20.total_ref, f32[32,32,128]{2,1,0:T(8,128)} %get-tuple-element.21.cols_ref, f32[32,8,128]{2,1,0:T(8,128)} %get-tuple-element.22.row_ref, f32[4]{0:T(128)} %skip_ref.1, ...), custom_call_target="tpu_custom_call" | custom-call | tf_op jit(solution)/shard_map/finish/pallas_call | solution.py:795
  101.1 2.3 %copy.16 = bf16[512,1024]{1,0:T(8,128)(2,1)} copy(bf16[512,1024]{1,0:T(8,128)(2,1)} %finish.1) | data formatting | bytes 2097152

commit v4 on v3

--- a/solution.py
+++ b/solution.py
@@ -140,17 +140,20 @@
 
     inner = vw_ref.shape[1]
     gain = gain_ref[...].reshape(1, -1)
-    for q in range(gate_ref.shape[0]):
-        at = slice(q * CHUNK, (q + 1) * CHUNK)
-        for r in range(0, CHUNK, 32):
-            rows[q * CHUNK + r : q * CHUNK + r + 32, :] = normalized(
-                h_ref[q * CHUNK + r : q * CHUNK + r + 32, :], gain
-            )
+    deep = min(256, h_ref.shape[0])
+    for first in range(0, h_ref.shape[0], deep):
+        for r in range(first, first + deep, 32):
+            rows[r : r + 32, :] = normalized(h_ref[r : r + 32, :], gain)
+        at = slice(first, first + deep)
         n = rows[at, :]
-        gate_ref[q, 0] = mm(n, gw_ref[...]).astype(bf16)
+        gate = mm(n, gw_ref[...]).astype(bf16)
         mix_ref[at, :inner] = mm(n, vw_ref[...]).astype(bf16)
         mix_ref[at, inner:] = mm(n, sw_ref[...]).astype(bf16)
-        raw_ref[q] = mm(turned[...], n, NT)
+        raw = mm(turned[...], n, NT)
+        for q in range(deep // CHUNK):
+            part = slice(q * CHUNK, (q + 1) * CHUNK)
+            gate_ref[first // CHUNK + q, 0] = gate[part]
+            raw_ref[first // CHUNK + q] = raw[:, part]
 
     @pl.when(i == pl.num_programs(0) - 1)
     def _():
@@ -333,6 +336,11 @@
         for k in range(CONV - 1):
             prod[k, b, at : at + values.shape[0], :] = values * taps[k : k + 1, lanes]
 
+    def ready(q):
+        for b in range(blocks):
+            lanes = slice(b * 128, (b + 1) * 128)
+            put(b, REACH + q * CHUNK, mix_ref[q * CHUNK : (q + 1) * CHUNK, lanes].astype(f32))
+
     def group(masked):
         for b in range(blocks):
             lanes = slice(b * 128, (b + 1) * 128)
@@ -340,9 +348,10 @@
             put(b, 0, jnp.where(g == 0, halo[HALO - REACH : HALO, lanes], ahead))
             behind = after_ref[:, lanes].astype(f32)[:REACH, :]
             put(b, REACH + rows, jnp.where(g == groups - 1, halo[HALO : HALO + REACH, lanes], behind))
-            for q in range(rounds):
-                put(b, REACH + q * CHUNK, mix_ref[q * CHUNK : (q + 1) * CHUNK, lanes].astype(f32))
+        ready(0)
         for q in range(rounds):
+            if q + 1 < rounds:
+                ready(q + 1)
             chunk(q, masked)
 
     def chunk(q, masked):
@@ -493,7 +502,6 @@
     gated,
     squares,
     others,
-    scales,
     sending,
     arrived,
     load,
@@ -579,6 +587,15 @@
         weigh(4, hop_hbm.at[0, top], 3 * inner, partner),
         weigh(5, hop_hbm.at[1, bottom], side + inner + half, partner),
     ]
+
+    def cross():
+        for copy in (u1, u2, t1, t3):
+            copy.wait_recv()
+        return [
+            weigh(6, weight.at[pl.ds(2 * inner + half, half)], 3 * inner + half, partner),
+            weigh(7, weight.at[pl.ds(side, half)], side + inner, partner),
+            weigh(8, weight.at[part(4)], 5 * inner, partner, inner),
+        ]
 
     i = lax.broadcasted_iota(jnp.int32, (CHUNK, CHUNK), 0)
     j = lax.broadcasted_iota(jnp.int32, (CHUNK, CHUNK), 1)
@@ -650,13 +667,6 @@
 
     for copy in travelling:
         copy.wait_recv()
-    for copy in (u1, u2, t1, t3):
-        copy.wait_recv()
-    beside += [
-        weigh(6, weight.at[pl.ds(2 * inner + half, half)], 3 * inner + half, partner),
-        weigh(7, weight.at[pl.ds(side, half)], side + inner, partner),
-        weigh(8, weight.at[part(4)], 5 * inner, partner, inner),
-    ]
     incoming[...] = jnp.zeros_like(incoming)
     for k in range(seq_count - 1, 0, -1):
 
@@ -675,15 +685,19 @@
     def passing(c):
         return jnp.exp2(head_lanes([cols_ref[c, h : h + 1, CHUNK - 1 :] for h in range(4)]))
 
-    def walk(c, carry):
-        b = chunks - 1 - c
-        for e, at in ((0, c), (1, b)):
-            state = incoming[e]
-            entry[e, at] = state.astype(bf16)
-            incoming[e] = state * passing(at) + fresh[at, e].astype(f32)
+    def walk(n, carry):
+        for e in range(2):
+            at = [2 * n, 2 * n + 1] if e == 0 else [chunks - 1 - 2 * n, chunks - 2 - 2 * n]
+            factors = [passing(c) for c in at]
+            for lanes in (slice(0, inner // 2), slice(inner // 2, inner)):
+                state = incoming[e, :, lanes]
+                for c, factor in zip(at, factors):
+                    entry[e, c, :, lanes] = state.astype(bf16)
+                    state = state * factor[:, lanes] + fresh[c, e, :, lanes].astype(f32)
+                incoming[e, :, lanes] = state
         return carry
 
-    lax.fori_loop(0, chunks, walk, 0)
+    lax.fori_loop(0, chunks // 2, walk, 0)
     gate_in.wait()
 
     ones = jnp.ones((8, inner), bf16)
@@ -713,24 +727,16 @@
         for k in range(1, head_count):
             total = total + others[q, k]
         total = lax.rsqrt(total * (1.0 / (inner * head_count)) + epsilon)
+        scale = jnp.concatenate([total, jnp.zeros((CHUNK - 2 * owners, CHUNK), f32)], axis=0).T
         for d in range(owners):
-            scales[q, d, 0:2, :] = total[2 * d : 2 * d + 2, :]
-        for k in range(head_count):
-            d = peers[k]
-            scale = jnp.concatenate(
-                [scales[q, d, 0:2, :], jnp.zeros((CHUNK - 2, CHUNK), f32)], axis=0
-            ).T
-            both = gated[q, d, :, :inner].astype(f32) * scale[:, 0:1]
-            both = both + gated[q, d, :, inner:].astype(f32) * scale[:, 1:2]
-            both = (both * gain).astype(bf16)
-            if k == 0:
-                arrived[q * CHUNK : (q + 1) * CHUNK, 0:inner] = both
-            else:
-                sending[q, k] = both
+            both = gated[q, d, :, :inner].astype(f32) * scale[:, 2 * d : 2 * d + 1]
+            both = both + gated[q, d, :, inner:].astype(f32) * scale[:, 2 * d + 1 : 2 * d + 2]
+            sending[q, d] = (both * gain).astype(bf16)
+        arrived[q * CHUNK : (q + 1) * CHUNK, 0:inner] = sending[q, head]
         return [
             start(
                 remote(
-                    sending.at[q, k],
+                    sending.at[q, peers[k]],
                     arrived.at[pl.ds(q * CHUNK, CHUNK), part(k)],
                     send.at[q, k],
                     recv.at[q, k],
@@ -742,9 +748,12 @@
 
     ss, pieces = [], []
     for q in range(rounds):
-        squares[q] = lax.fori_loop(
-            0, owners, lambda d, sums, q=q: carried(q, d, sums), jnp.zeros((2 * owners, CHUNK), f32)
-        )
+        def some(n, sums, q=q):
+            for u in range(4):
+                sums = carried(q, 4 * n + u, sums)
+            return sums
+
+        squares[q] = lax.fori_loop(0, owners // 4, some, jnp.zeros((2 * owners, CHUNK), f32))
         ss.append(
             [
                 start(
@@ -757,6 +766,8 @@
         )
         if q:
             pieces.append(combine(q - 1))
+        if q == 0:
+            beside += cross()
     pieces.append(combine(rounds - 1))
 
     for copy in late:
@@ -821,7 +832,6 @@
             pltpu.VMEM((rounds, owners, CHUNK, 2 * inner), bf16),
             pltpu.VMEM((rounds, 2 * owners, CHUNK), f32),
             pltpu.VMEM((rounds, head_count, 2 * owners, CHUNK), f32),
-            pltpu.VMEM((rounds, owners, 8, CHUNK), f32),
             pltpu.VMEM((rounds, head_count, CHUNK, inner), bf16),
             pltpu.VMEM((rows, head_count * inner), bf16),
             dma((rounds + 7,)),

time: 105 us -> 102 us (0.971)
  Pallas kernels: 101 us -> 98.8 us
    pallas_call x1, Pallas kernels: 63.7 us -> 61.2 us  [finish(): pl.pallas_call(functools.partial(finish_kernel, seq_count, head_count), i...]
where the time goes in v4:
time: 102 us; the launch traced here: 101 us
  Pallas kernels  98.8 us (97%)
  local copies, waits for them, and re-layouts  2.26 us (2%)
    pallas_call x1, Pallas kernels, finish(): pl.pallas_call(functools.partial(finish_kernel, seq_count, head_count), i...  61.2 us
    pallas_call x1, Pallas kernels, project(): pl.pallas_call(functools.partial(project_kernel, mesh_shape), grid=(token...  19.4 us
    pallas_call x1, Pallas kernels, states(): pl.pallas_call(functools.partial(states_kernel, axis), grid=(owners,), in...  18.1 us
    unnamed x1, local copies, waits for them, and re-layouts  2.26 us

profile of v4, /device:TPU:1, one launch (start us, length us, event | category | flops | bytes accessed | tf_op | source)
XLA Modules:
  0.0 101.1 jit_solution(3142280544032893295)
XLA Ops:
  0.0 19.4 %project.1 = (bf16[4,8,128,256]{3,2,1,0:T(8,128)(2,1)}, bf16[4096,512]{1,0:T(8,128)(2,1)}, f32[32,8,128]{2,1,0:T(8,128)}, bf16[32,1024]{1,0:T(8,128)(2,1)}, bf16[3,256,1024]{2,1,0:T(8,128)(2,1)}) custom-call(bf16[4096,1024]{1,0:T(8,128)(2,1)} %hidden_hbm.1, bf16[1024]{0:T(1024)(128)(2,1)} %gain_ref.4, bf16[1024,256]{1,0:T(8,128)(2,1)} %gw_ref.1, ...), custom_call_target="tpu_custom_call" | custom-call | tf_op jit(solution)/shard_map/project/pallas_call | solution.py:170
  19.4 18.1 %states.1 = (bf16[4,8,128,1024]{3,2,1,0:T(8,128)(2,1)}, bf16[32,2,128,256]{3,2,1,0:T(8,128)(2,1)}, f32[32,32,128]{2,1,0:T(8,128)}, f32[32,8,128]{2,1,0:T(8,128)}...) custom-call(bf16[4096,512]{1,0:T(8,128)(2,1)} %get-tuple-element.16.mix_ref.before_ref.after_ref, ...), custom_call_target="tpu_custom_call" | custom-call | tf_op jit(solution)/shard_map/states/pallas_call | solution.py:419
  37.6 61.2 %finish.1 = bf16[512,1024]{1,0:T(8,128)(2,1)} custom-call(bf16[2,128,256]{2,1,0:T(8,128)(2,1)} %get-tuple-element.19.end_ref, f32[8,256]{1,0:T(8,128)} %get-tuple-element.20.total_ref, f32[32,32,128]{2,1,0:T(8,128)} %get-tuple-element.21.cols_ref, f32[32,8,128]{2,1,0:T(8,128)} %get-tuple-element.22.row_ref, f32[4]{0:T(128)} %skip_ref.1, ...), custom_call_target="tpu_custom_call" | custom-call | tf_op jit(solution)/shard_map/finish/pallas_call | solution.py:806
  98.8 2.3 %copy.16 = bf16[512,1024]{1,0:T(8,128)(2,1)} copy(bf16[512,1024]{1,0:T(8,128)(2,1)} %finish.1) | data formatting | bytes 2097152

commit v5 on v4

--- a/solution.py
+++ b/solution.py
@@ -105,13 +105,12 @@
     mesh_shape,
     h_ref,
     gain_ref,
-    gw_ref,
     vw_ref,
     sw_ref,
     tw_ref,
     hidden,
     w,
-    gate_ref,
+    norm_ref,
     mix_ref,
     raw_ref,
     halo,
@@ -143,17 +142,16 @@
     deep = min(256, h_ref.shape[0])
     for first in range(0, h_ref.shape[0], deep):
         for r in range(first, first + deep, 32):
-            rows[r : r + 32, :] = normalized(h_ref[r : r + 32, :], gain)
+            n = normalized(h_ref[r : r + 32, :], gain)
+            rows[r : r + 32, :] = n
+            norm_ref[r // CHUNK, 0, r % CHUNK : r % CHUNK + 32, :] = n
         at = slice(first, first + deep)
         n = rows[at, :]
-        gate = mm(n, gw_ref[...]).astype(bf16)
         mix_ref[at, :inner] = mm(n, vw_ref[...]).astype(bf16)
         mix_ref[at, inner:] = mm(n, sw_ref[...]).astype(bf16)
         raw = mm(turned[...], n, NT)
         for q in range(deep // CHUNK):
-            part = slice(q * CHUNK, (q + 1) * CHUNK)
-            gate_ref[first // CHUNK + q, 0] = gate[part]
-            raw_ref[first // CHUNK + q] = raw[:, part]
+            raw_ref[first // CHUNK + q] = raw[:, q * CHUNK : (q + 1) * CHUNK]
 
     @pl.when(i == pl.num_programs(0) - 1)
     def _():
@@ -161,7 +159,7 @@
             copy.wait()
 
 
-def project(mesh_shape, hidden, gain, gw, vw, sw, tw, w):
+def project(mesh_shape, hidden, gain, vw, sw, tw, w):
     tokens, width = hidden.shape
     inner = vw.shape[1]
     mixed = inner + sw.shape[1]
@@ -173,7 +171,6 @@
         in_specs=[
             pl.BlockSpec((rows, width), lambda i: (i, 0)),
             whole(gain.shape),
-            whole(gw.shape),
             whole(vw.shape),
             whole(sw.shape),
             whole(tw.shape),
@@ -181,14 +178,14 @@
             ANY_SPEC,
         ],
         out_specs=[
-            pl.BlockSpec((rounds, 1, CHUNK, inner), lambda i: (0, i, 0, 0)),
+            pl.BlockSpec((rounds, 1, CHUNK, width), lambda i: (0, i, 0, 0)),
             pl.BlockSpec((rows, mixed), lambda i: (i, 0)),
             pl.BlockSpec((rows // CHUNK, 8, CHUNK), lambda i: (i, 0, 0)),
             ANY_SPEC,
             ANY_SPEC,
         ],
         out_shape=[
-            jax.ShapeDtypeStruct((rounds, tokens // rows, CHUNK, inner), bf16),
+            jax.ShapeDtypeStruct((rounds, tokens // rows, CHUNK, width), bf16),
             jax.ShapeDtypeStruct((tokens, mixed), bf16),
             jax.ShapeDtypeStruct((tokens // CHUNK, 8, CHUNK), f32),
             jax.ShapeDtypeStruct((2 * HALO, width), bf16),
@@ -202,7 +199,7 @@
         ],
         compiler_params=params(collective_id=2, has_side_effects=True),
         name="project",
-    )(hidden, gain, gw, vw, sw, tw, hidden, w)
+    )(hidden, gain, vw, sw, tw, hidden, w)
 
 
 def head_lanes(columns):
@@ -480,14 +477,16 @@
     row_ref,
     skip_ref,
     gain_ref,
+    gw_ref,
     conv_hbm,
-    gate_hbm,
+    norm_hbm,
     fresh_hbm,
     hidden_hbm,
     w_hbm,
     hop_hbm,
     out_ref,
     conv,
+    normed,
     gate,
     fresh,
     rest,
@@ -534,9 +533,11 @@
     def part(k):
         return pl.ds(k * inner, inner)
 
-    conv_in = [fetch(conv_hbm.at[q], conv.at[q], q) for q in range(rounds)]
+    conv_in, norm_in = [], []
+    for q in range(rounds):
+        conv_in.append(fetch(conv_hbm.at[q], conv.at[q], q))
+        norm_in.append(fetch(norm_hbm.at[q], normed.at[q], rounds + 7 + q))
     fresh_in = fetch(fresh_hbm, fresh, rounds)
-    gate_in = fetch(gate_hbm, gate, rounds + 1)
     mine = pl.ds(pl.multiple_of(head * rows, rows), rows)
     half = inner // 2
     side = (2 * chips - 2) * inner
@@ -655,10 +656,19 @@
                 made_here = made_here + skip[:, p * CHUNK : (p + 1) * CHUNK] * x.astype(f32)
                 inside[q, d, :, e * inner + p * CHUNK : e * inner + (p + 1) * CHUNK] = made_here
 
+    def gates(q, n):
+        two = normed[q, pl.ds(2 * n, 2)].reshape(2 * CHUNK, normed.shape[3])
+        two = mm(two, gw_ref[...]).astype(bf16)
+        for u in range(2):
+            gate[q, 2 * n + u] = two[u * CHUNK : (u + 1) * CHUNK]
+
     for q in range(rounds):
         conv_in[q].wait()
+        norm_in[q].wait()
 
         def step(n, carry, q=q):
+            if q < 2:
+                gates(q, n)
             for u in range(2):
                 within(q, 2 * n + u, u)
             return carry
@@ -698,7 +708,6 @@
         return carry
 
     lax.fori_loop(0, chunks // 2, walk, 0)
-    gate_in.wait()
 
     ones = jnp.ones((8, inner), bf16)
     gain = gain_ref[...].reshape(1, -1).astype(f32)
@@ -748,6 +757,14 @@
 
     ss, pieces = [], []
     for q in range(rounds):
+        if q >= 2:
+
+            def later(n, carry, q=q):
+                gates(q, n)
+                return carry
+
+            lax.fori_loop(0, owners // 2, later, 0)
+
         def some(n, sums, q=q):
             for u in range(4):
                 sums = carried(q, 4 * n + u, sums)
@@ -796,11 +813,11 @@
         copy.wait_send()
 
 
-def finish(mesh_shape, end, total, cols, row, skip, gain, conv, gate, fresh, hidden, w, hop):
+def finish(mesh_shape, end, total, cols, row, skip, gain, gw, conv, normed, fresh, hidden, w, hop):
     seq_count, head_count = mesh_shape
     rounds, owners = conv.shape[:2]
     rows = rounds * CHUNK
-    inner = gate.shape[3]
+    inner = gw.shape[1]
     width = hidden.shape[1]
     dma = pltpu.SemaphoreType.DMA
     return pl.pallas_call(
@@ -812,13 +829,15 @@
             whole(row.shape),
             SMEM_SPEC,
             whole(gain.shape),
+            whole(gw.shape),
         ]
         + [ANY_SPEC] * 6,
         out_specs=whole((rows, width)),
         out_shape=jax.ShapeDtypeStruct((rows, width), bf16),
         scratch_shapes=[
             pltpu.VMEM(conv.shape, bf16),
-            pltpu.VMEM(gate.shape, bf16),
+            pltpu.VMEM(normed.shape, bf16),
+            pltpu.VMEM((rounds, owners, CHUNK, inner), bf16),
             pltpu.VMEM(fresh.shape, bf16),
             pltpu.VMEM((rows, width), bf16),
             pltpu.VMEM((head_count * inner, width), bf16),
@@ -834,7 +853,7 @@
             pltpu.VMEM((rounds, head_count, 2 * owners, CHUNK), f32),
             pltpu.VMEM((rounds, head_count, CHUNK, inner), bf16),
             pltpu.VMEM((rows, head_count * inner), bf16),
-            dma((rounds + 7,)),
+            dma((2 * rounds + 7,)),
             dma((2, seq_count)),
             dma((2, seq_count)),
             dma((9,)),
@@ -846,7 +865,7 @@
         ],
         compiler_params=params(collective_id=1, has_side_effects=True),
         name="finish",
-    )(end, total, cols, row, skip, gain, conv, gate, fresh, hidden, w, hop)
+    )(end, total, cols, row, skip, gain, gw, conv, normed, fresh, hidden, w, hop)
 
 
 def local(
@@ -867,8 +886,8 @@
 ):
     seq_count, head_count = lax.axis_size("seq"), lax.axis_size("head")
     shape = (seq_count, head_count)
-    gate, mix, raw, halo, hop = project(
-        shape, hidden_in, norm_gain, gate_weight, value_weight, state_weight, step_weight.T, output_weight
+    normed, mix, raw, halo, hop = project(
+        shape, hidden_in, norm_gain, value_weight, state_weight, step_weight.T, output_weight
     )
     conv, fresh, cols, row, end, total = states(
         "seq",
@@ -893,8 +912,9 @@
         row,
         skip_gain,
         output_gain,
+        gate_weight,
         conv,
-        gate,
+        normed,
         fresh,
         hidden_in,
         output_weight,

time: 102 us -> 101 us (level)
  no operation moved by 1% of the time
where the time goes in v5:
time: 101 us
  Pallas kernels  98.6 us (98%)
  local copies, waits for them, and re-layouts  2.26 us (2%)
    pallas_call x1, Pallas kernels, finish(): pl.pallas_call(functools.partial(finish_kernel, seq_count, head_count), i...  61 us
    pallas_call x1, Pallas kernels, project(): pl.pallas_call(functools.partial(project_kernel, mesh_shape), grid=(token...  19.5 us
    pallas_call x1, Pallas kernels, states(): pl.pallas_call(functools.partial(states_kernel, axis), grid=(owners,), in...  18.1 us
    unnamed x1, local copies, waits for them, and re-layouts  2.26 us

profile of v5, /device:TPU:1, one launch (start us, length us, event | category | flops | bytes accessed | tf_op | source)
XLA Modules:
  0.0 100.9 jit_solution(16375678183303247320)
XLA Ops:
  0.0 19.5 %project.1 = (bf16[4,8,128,1024]{3,2,1,0:T(8,128)(2,1)}, bf16[4096,512]{1,0:T(8,128)(2,1)}, f32[32,8,128]{2,1,0:T(8,128)}, bf16[32,1024]{1,0:T(8,128)(2,1)}, bf16[3,256,1024]{2,1,0:T(8,128)(2,1)}) custom-call(bf16[4096,1024]{1,0:T(8,128)(2,1)} %hidden_hbm.1, bf16[1024]{0:T(1024)(128)(2,1)} %gain_ref.4, bf16[1024,256]{1,0:T(8,128)(2,1)} %vw_ref.3, ...), custom_call_target="tpu_custom_call" | custom-call | tf_op jit(solution)/shard_map/project/pallas_call | solution.py:168
  19.5 18.1 %states.1 = (bf16[4,8,128,1024]{3,2,1,0:T(8,128)(2,1)}, bf16[32,2,128,256]{3,2,1,0:T(8,128)(2,1)}, f32[32,32,128]{2,1,0:T(8,128)}, f32[32,8,128]{2,1,0:T(8,128)}...) custom-call(bf16[4096,512]{1,0:T(8,128)(2,1)} %get-tuple-element.16.mix_ref.before_ref.after_ref, ...), custom_call_target="tpu_custom_call" | custom-call | tf_op jit(solution)/shard_map/states/pallas_call | solution.py:416
  37.6 61.0 %finish.1 = bf16[512,1024]{1,0:T(8,128)(2,1)} custom-call(bf16[2,128,256]{2,1,0:T(8,128)(2,1)} %get-tuple-element.19.end_ref, f32[8,256]{1,0:T(8,128)} %get-tuple-element.20.total_ref, f32[32,32,128]{2,1,0:T(8,128)} %get-tuple-element.21.cols_ref, f32[32,8,128]{2,1,0:T(8,128)} %get-tuple-element.22.row_ref, f32[4]{0:T(128)} %skip_ref.1, ...), custom_call_target="tpu_custom_call" | custom-call | tf_op jit(solution)/shard_map/finish/pallas_call | solution.py:823
  98.7 2.3 %copy.16 = bf16[512,1024]{1,0:T(8,128)(2,1)} copy(bf16[512,1024]{1,0:T(8,128)(2,1)} %finish.1) | data formatting | bytes 2097152

commit v6 on v5

--- a/solution.py
+++ b/solution.py
@@ -78,50 +78,38 @@
     return ((y + dy) % chips) * 2 + (core + dc) % 2
 
 
-def project_copies(seq_count, head_count, hidden, w, halo, hop, send, recv):
+def project_copies(seq_count, hidden, halo, send, recv):
     me = lax.axis_index("seq")
-    head = lax.axis_index("head")
-    chips = head_count // 2
     tokens = hidden.shape[0]
     after = (me + 1) % seq_count
     before = (me + seq_count - 1) % seq_count
     first, last = pl.ds(0, HALO), pl.ds(tokens - HALO, HALO)
     low, high = pl.ds(0, HALO), pl.ds(HALO, HALO)
-    half = w.shape[0] // 2
-    top, bottom = pl.ds(0, half), pl.ds(half, half)
-    up = head_peer(head, chips, 1, 0)
-    down = head_peer(head, chips, chips - 1, 0)
-    partner = head_peer(head, chips, 0, 1)
     return (
         remote(hidden.at[last], halo.at[low], send.at[0], recv.at[0], seq=after),
         remote(hidden.at[first], halo.at[high], send.at[1], recv.at[1], seq=before),
-        remote(w.at[top], hop.at[0, top], send.at[2], recv.at[2], head=up),
-        remote(w.at[bottom], hop.at[1, bottom], send.at[3], recv.at[3], head=down),
-        remote(w, hop.at[2], send.at[4], recv.at[4], head=partner),
-    ), [{"seq": after}, {"seq": before}, {"head": up}, {"head": down}, {"head": partner}]
+    ), [{"seq": after}, {"seq": before}]
 
 
 def project_kernel(
-    mesh_shape,
+    seq_count,
     h_ref,
     gain_ref,
     vw_ref,
     sw_ref,
     tw_ref,
     hidden,
-    w,
     norm_ref,
     mix_ref,
     raw_ref,
     halo,
-    hop,
     turned,
     rows,
     send,
     recv,
 ):
     i = pl.program_id(0)
-    copies, peers = project_copies(*mesh_shape, hidden, w, halo, hop, send, recv)
+    copies, peers = project_copies(seq_count, hidden, halo, send, recv)
     barrier = pltpu.get_barrier_semaphore()
 
     @pl.when(i == 0)
@@ -159,14 +147,14 @@
             copy.wait()
 
 
-def project(mesh_shape, hidden, gain, vw, sw, tw, w):
+def project(mesh_shape, hidden, gain, vw, sw, tw):
     tokens, width = hidden.shape
     inner = vw.shape[1]
     mixed = inner + sw.shape[1]
     rows = tokens // mesh_shape[1]
     rounds = rows // CHUNK
     return pl.pallas_call(
-        functools.partial(project_kernel, mesh_shape),
+        functools.partial(project_kernel, mesh_shape[0]),
         grid=(tokens // rows,),
         in_specs=[
             pl.BlockSpec((rows, width), lambda i: (i, 0)),
@@ -175,13 +163,11 @@
             whole(sw.shape),
             whole(tw.shape),
             ANY_SPEC,
-            ANY_SPEC,
         ],
         out_specs=[
             pl.BlockSpec((rounds, 1, CHUNK, width), lambda i: (0, i, 0, 0)),
             pl.BlockSpec((rows, mixed), lambda i: (i, 0)),
             pl.BlockSpec((rows // CHUNK, 8, CHUNK), lambda i: (i, 0, 0)),
-            ANY_SPEC,
             ANY_SPEC,
         ],
         out_shape=[
@@ -189,17 +175,16 @@
             jax.ShapeDtypeStruct((tokens, mixed), bf16),
             jax.ShapeDtypeStruct((tokens // CHUNK, 8, CHUNK), f32),
             jax.ShapeDtypeStruct((2 * HALO, width), bf16),
-            jax.ShapeDtypeStruct((3,) + w.shape, bf16),
         ],
         scratch_shapes=[
             pltpu.VMEM((8, width), bf16),
             pltpu.VMEM((rows, width), bf16),
-            pltpu.SemaphoreType.DMA((5,)),
-            pltpu.SemaphoreType.DMA((5,)),
+            pltpu.SemaphoreType.DMA((2,)),
+            pltpu.SemaphoreType.DMA((2,)),
         ],
         compiler_params=params(collective_id=2, has_side_effects=True),
         name="project",
-    )(hidden, gain, vw, sw, tw, hidden, w)
+    )(hidden, gain, vw, sw, tw, hidden)
 
 
 def head_lanes(columns):
@@ -483,7 +468,6 @@
     fresh_hbm,
     hidden_hbm,
     w_hbm,
-    hop_hbm,
     out_ref,
     conv,
     normed,
@@ -546,9 +530,6 @@
     late = [
         fetch(hidden_hbm.at[mine, :], rest, rounds + 2),
         fetch(w_hbm, weight.at[part(0)], rounds + 3),
-        fetch(hop_hbm.at[2], weight.at[part(1)], rounds + 4),
-        fetch(hop_hbm.at[0, top], weight.at[pl.ds(2 * inner, half)], rounds + 5),
-        fetch(hop_hbm.at[1, bottom], weight.at[pl.ds(side + half, half)], rounds + 6),
     ]
 
     greet(
@@ -580,22 +561,25 @@
         at = weight.at[pl.ds(row, count)]
         return start(remote(src, at, w_send.at[n], w_recv.at[n], head=where))
 
-    u1 = weigh(0, w_hbm.at[bottom], 2 * inner + half, up)
-    u2 = weigh(1, w_hbm.at[top], side, down)
-    t1 = weigh(2, hop_hbm.at[0, top], far, up)
-    t3 = weigh(3, hop_hbm.at[1, bottom], far + half, down)
-    beside = [
-        weigh(4, hop_hbm.at[0, top], 3 * inner, partner),
-        weigh(5, hop_hbm.at[1, bottom], side + inner + half, partner),
-    ]
+    u1 = weigh(0, w_hbm.at[top], 2 * inner, up)
+    u2 = weigh(1, w_hbm.at[bottom], side + half, down)
+    u3 = weigh(2, w_hbm.at[bottom], 2 * inner + half, up)
+    u4 = weigh(3, w_hbm.at[top], side, down)
+    beside = [weigh(4, w_hbm, inner, partner, inner)]
+
+    def onward():
+        u1.wait_recv()
+        t1 = weigh(5, weight.at[pl.ds(2 * inner, half)], far, up)
+        u2.wait_recv()
+        return t1, weigh(6, weight.at[pl.ds(side + half, half)], far + half, down)
 
     def cross():
-        for copy in (u1, u2, t1, t3):
+        for copy in (u3, u4) + second:
             copy.wait_recv()
         return [
-            weigh(6, weight.at[pl.ds(2 * inner + half, half)], 3 * inner + half, partner),
-            weigh(7, weight.at[pl.ds(side, half)], side + inner, partner),
-            weigh(8, weight.at[part(4)], 5 * inner, partner, inner),
+            weigh(7, weight.at[part(2)], 3 * inner, partner, inner),
+            weigh(8, weight.at[part(2 * chips - 2)], side + inner, partner, inner),
+            weigh(9, weight.at[part(4)], 5 * inner, partner, inner),
         ]
 
     i = lax.broadcasted_iota(jnp.int32, (CHUNK, CHUNK), 0)
@@ -675,6 +659,8 @@
 
         lax.fori_loop(0, owners // 2, step, 0)
 
+    second = onward()
+
     for copy in travelling:
         copy.wait_recv()
     incoming[...] = jnp.zeros_like(incoming)
@@ -813,7 +799,7 @@
         copy.wait_send()
 
 
-def finish(mesh_shape, end, total, cols, row, skip, gain, gw, conv, normed, fresh, hidden, w, hop):
+def finish(mesh_shape, end, total, cols, row, skip, gain, gw, conv, normed, fresh, hidden, w):
     seq_count, head_count = mesh_shape
     rounds, owners = conv.shape[:2]
     rows = rounds * CHUNK
@@ -831,7 +817,7 @@
             whole(gain.shape),
             whole(gw.shape),
         ]
-        + [ANY_SPEC] * 6,
+        + [ANY_SPEC] * 5,
         out_specs=whole((rows, width)),
         out_shape=jax.ShapeDtypeStruct((rows, width), bf16),
         scratch_shapes=[
@@ -856,8 +842,8 @@
             dma((2 * rounds + 7,)),
             dma((2, seq_count)),
             dma((2, seq_count)),
-            dma((9,)),
-            dma((9,)),
+            dma((10,)),
+            dma((10,)),
             dma((rounds, head_count)),
             dma((rounds, head_count)),
             dma((rounds, head_count)),
@@ -865,7 +851,7 @@
         ],
         compiler_params=params(collective_id=1, has_side_effects=True),
         name="finish",
-    )(end, total, cols, row, skip, gain, gw, conv, normed, fresh, hidden, w, hop)
+    )(end, total, cols, row, skip, gain, gw, conv, normed, fresh, hidden, w)
 
 
 def local(
@@ -886,8 +872,8 @@
 ):
     seq_count, head_count = lax.axis_size("seq"), lax.axis_size("head")
     shape = (seq_count, head_count)
-    normed, mix, raw, halo, hop = project(
-        shape, hidden_in, norm_gain, value_weight, state_weight, step_weight.T, output_weight
+    normed, mix, raw, halo = project(
+        shape, hidden_in, norm_gain, value_weight, state_weight, step_weight.T
     )
     conv, fresh, cols, row, end, total = states(
         "seq",
@@ -918,7 +904,6 @@
         fresh,
         hidden_in,
         output_weight,
-        hop,
     )
 
 

time: 101 us -> 102 us (level)
  no operation moved by 1% of the time
where the time goes in v6:
time: 102 us; the launch traced here: 101 us
  Pallas kernels  99 us (97%)
  local copies, waits for them, and re-layouts  2.26 us (2%)
    pallas_call x1, Pallas kernels, finish(): pl.pallas_call(functools.partial(finish_kernel, seq_count, head_count), i...  61.8 us
    pallas_call x1, Pallas kernels, project(): pl.pallas_call(functools.partial(project_kernel, mesh_shape[0]), grid=(to...  19.4 us
    pallas_call x1, Pallas kernels, states(): pl.pallas_call(functools.partial(states_kernel, axis), grid=(owners,), in...  17.7 us
    unnamed x1, local copies, waits for them, and re-layouts  2.26 us

profile of v6, /device:TPU:1, one launch (start us, length us, event | category | flops | bytes accessed | tf_op | source)
XLA Modules:
  0.0 101.3 jit_solution(12154611519820592479)
XLA Ops:
  0.0 19.4 %project.1 = (bf16[4,8,128,1024]{3,2,1,0:T(8,128)(2,1)}, bf16[4096,512]{1,0:T(8,128)(2,1)}, f32[32,8,128]{2,1,0:T(8,128)}, bf16[32,1024]{1,0:T(8,128)(2,1)}) custom-call(bf16[4096,1024]{1,0:T(8,128)(2,1)} %hidden_hbm.1, bf16[1024]{0:T(1024)(128)(2,1)} %gain_ref.4, bf16[1024,256]{1,0:T(8,128)(2,1)} %vw_ref.3, bf16[1024,256]{1,0:T(8,128)(2,1)} %sw_ref.3, ...), custom_call_target="tpu_custom_call" | custom-call | tf_op jit(solution)/shard_map/project/pallas_call | solution.py:156
  19.4 17.7 %states.1 = (bf16[4,8,128,1024]{3,2,1,0:T(8,128)(2,1)}, bf16[32,2,128,256]{3,2,1,0:T(8,128)(2,1)}, f32[32,32,128]{2,1,0:T(8,128)}, f32[32,8,128]{2,1,0:T(8,128)}...) custom-call(bf16[4096,512]{1,0:T(8,128)(2,1)} %get-tuple-element.15.mix_ref.before_ref.after_ref, ...), custom_call_target="tpu_custom_call" | custom-call | tf_op jit(solution)/shard_map/states/pallas_call | solution.py:401
  37.2 61.8 %finish.1 = bf16[512,1024]{1,0:T(8,128)(2,1)} custom-call(bf16[2,128,256]{2,1,0:T(8,128)(2,1)} %get-tuple-element.18.end_ref, f32[8,256]{1,0:T(8,128)} %get-tuple-element.19.total_ref, f32[32,32,128]{2,1,0:T(8,128)} %get-tuple-element.20.cols_ref, f32[32,8,128]{2,1,0:T(8,128)} %get-tuple-element.21.row_ref, f32[4]{0:T(128)} %skip_ref.1, ...), custom_call_target="tpu_custom_call" | custom-call | tf_op jit(solution)/shard_map/finish/pallas_call | solution.py:809
  99.0 2.3 %copy.16 = bf16[512,1024]{1,0:T(8,128)(2,1)} copy(bf16[512,1024]{1,0:T(8,128)(2,1)} %finish.1) | data formatting | bytes 2097152

commit v7 on v5

--- a/solution.py
+++ b/solution.py
@@ -110,7 +110,6 @@
     tw_ref,
     hidden,
     w,
-    norm_ref,
     mix_ref,
     raw_ref,
     halo,
@@ -142,9 +141,7 @@
     deep = min(256, h_ref.shape[0])
     for first in range(0, h_ref.shape[0], deep):
         for r in range(first, first + deep, 32):
-            n = normalized(h_ref[r : r + 32, :], gain)
-            rows[r : r + 32, :] = n
-            norm_ref[r // CHUNK, 0, r % CHUNK : r % CHUNK + 32, :] = n
+            rows[r : r + 32, :] = normalized(h_ref[r : r + 32, :], gain)
         at = slice(first, first + deep)
         n = rows[at, :]
         mix_ref[at, :inner] = mm(n, vw_ref[...]).astype(bf16)
@@ -164,7 +161,6 @@
     inner = vw.shape[1]
     mixed = inner + sw.shape[1]
     rows = tokens // mesh_shape[1]
-    rounds = rows // CHUNK
     return pl.pallas_call(
         functools.partial(project_kernel, mesh_shape),
         grid=(tokens // rows,),
@@ -178,14 +174,12 @@
             ANY_SPEC,
         ],
         out_specs=[
-            pl.BlockSpec((rounds, 1, CHUNK, width), lambda i: (0, i, 0, 0)),
             pl.BlockSpec((rows, mixed), lambda i: (i, 0)),
             pl.BlockSpec((rows // CHUNK, 8, CHUNK), lambda i: (i, 0, 0)),
             ANY_SPEC,
             ANY_SPEC,
         ],
         out_shape=[
-            jax.ShapeDtypeStruct((rounds, tokens // rows, CHUNK, width), bf16),
             jax.ShapeDtypeStruct((tokens, mixed), bf16),
             jax.ShapeDtypeStruct((tokens // CHUNK, 8, CHUNK), f32),
             jax.ShapeDtypeStruct((2 * HALO, width), bf16),
@@ -478,15 +472,15 @@
     skip_ref,
     gain_ref,
     gw_ref,
+    norm_gain_ref,
     conv_hbm,
-    norm_hbm,
     fresh_hbm,
     hidden_hbm,
     w_hbm,
     hop_hbm,
     out_ref,
     conv,
-    normed,
+    wide,
     gate,
     fresh,
     rest,
@@ -533,18 +527,17 @@
     def part(k):
         return pl.ds(k * inner, inner)
 
-    conv_in, norm_in = [], []
+    conv_in, wide_in = [], []
     for q in range(rounds):
         conv_in.append(fetch(conv_hbm.at[q], conv.at[q], q))
-        norm_in.append(fetch(norm_hbm.at[q], normed.at[q], rounds + 7 + q))
+        wide_in.append(fetch(hidden_hbm.at[:, q], wide.at[q], rounds + 7 + q))
     fresh_in = fetch(fresh_hbm, fresh, rounds)
-    mine = pl.ds(pl.multiple_of(head * rows, rows), rows)
     half = inner // 2
     side = (2 * chips - 2) * inner
     far = 4 * inner
     top, bottom = pl.ds(0, half), pl.ds(half, half)
     late = [
-        fetch(hidden_hbm.at[mine, :], rest, rounds + 2),
+        fetch(hidden_hbm.at[head], rest, rounds + 2),
         fetch(w_hbm, weight.at[part(0)], rounds + 3),
         fetch(hop_hbm.at[2], weight.at[part(1)], rounds + 4),
         fetch(hop_hbm.at[0, top], weight.at[pl.ds(2 * inner, half)], rounds + 5),
@@ -657,14 +650,14 @@
                 inside[q, d, :, e * inner + p * CHUNK : e * inner + (p + 1) * CHUNK] = made_here
 
     def gates(q, n):
-        two = normed[q, pl.ds(2 * n, 2)].reshape(2 * CHUNK, normed.shape[3])
-        two = mm(two, gw_ref[...]).astype(bf16)
+        two = wide[q, pl.ds(2 * n, 2)].reshape(2 * CHUNK, wide.shape[3])
+        two = mm(normalized(two, norm_gain_ref[...].reshape(1, -1)), gw_ref[...]).astype(bf16)
         for u in range(2):
             gate[q, 2 * n + u] = two[u * CHUNK : (u + 1) * CHUNK]
 
     for q in range(rounds):
         conv_in[q].wait()
-        norm_in[q].wait()
+        wide_in[q].wait()
 
         def step(n, carry, q=q):
             if q < 2:
@@ -803,8 +796,9 @@
             def project_out(b, carry, first=first, count=count):
                 lanes = pl.ds(pl.multiple_of(b * step_lanes, step_lanes), step_lanes)
                 here = pl.ds(first, count)
+                of = pl.ds(first // CHUNK, count // CHUNK)
                 out_ref[here, lanes] = (
-                    mm(arrived[here, :], weight[:, lanes]) + rest[here, lanes].astype(f32)
+                    mm(arrived[here, :], weight[:, lanes]) + rest[of, :, lanes].reshape(count, step_lanes).astype(f32)
                 ).astype(bf16)
                 return carry
 
@@ -813,12 +807,12 @@
         copy.wait_send()
 
 
-def finish(mesh_shape, end, total, cols, row, skip, gain, gw, conv, normed, fresh, hidden, w, hop):
+def finish(mesh_shape, end, total, cols, row, skip, gain, gw, norm_gain, conv, fresh, hidden, w, hop):
     seq_count, head_count = mesh_shape
     rounds, owners = conv.shape[:2]
     rows = rounds * CHUNK
     inner = gw.shape[1]
-    width = hidden.shape[1]
+    width = hidden.shape[3]
     dma = pltpu.SemaphoreType.DMA
     return pl.pallas_call(
         functools.partial(finish_kernel, seq_count, head_count),
@@ -830,16 +824,17 @@
             SMEM_SPEC,
             whole(gain.shape),
             whole(gw.shape),
+            whole(norm_gain.shape),
         ]
-        + [ANY_SPEC] * 6,
+        + [ANY_SPEC] * 5,
         out_specs=whole((rows, width)),
         out_shape=jax.ShapeDtypeStruct((rows, width), bf16),
         scratch_shapes=[
             pltpu.VMEM(conv.shape, bf16),
-            pltpu.VMEM(normed.shape, bf16),
+            pltpu.VMEM((rounds, owners, CHUNK, width), bf16),
             pltpu.VMEM((rounds, owners, CHUNK, inner), bf16),
             pltpu.VMEM(fresh.shape, bf16),
-            pltpu.VMEM((rows, width), bf16),
+            pltpu.VMEM((rounds, CHUNK, width), bf16),
             pltpu.VMEM((head_count * inner, width), bf16),
             pltpu.VMEM((seq_count,) + end.shape[1:], bf16),
             pltpu.VMEM((seq_count,) + total.shape, f32),
@@ -865,7 +860,7 @@
         ],
         compiler_params=params(collective_id=1, has_side_effects=True),
         name="finish",
-    )(end, total, cols, row, skip, gain, gw, conv, normed, fresh, hidden, w, hop)
+    )(end, total, cols, row, skip, gain, gw, norm_gain, conv, fresh, hidden, w, hop)
 
 
 def local(
@@ -886,7 +881,7 @@
 ):
     seq_count, head_count = lax.axis_size("seq"), lax.axis_size("head")
     shape = (seq_count, head_count)
-    normed, mix, raw, halo, hop = project(
+    mix, raw, halo, hop = project(
         shape, hidden_in, norm_gain, value_weight, state_weight, step_weight.T, output_weight
     )
     conv, fresh, cols, row, end, total = states(
@@ -913,10 +908,10 @@
         skip_gain,
         output_gain,
         gate_weight,
+        norm_gain,
         conv,
-        normed,
         fresh,
-        hidden_in,
+        hidden_in.reshape(head_count, -1, CHUNK, hidden_in.shape[1]),
         output_weight,
         hop,
     )

time: 101 us -> 100 us (0.990)
    pallas_call x1, Pallas kernels: 19.5 us -> 18 us  [project(): pl.pallas_call(functools.partial(project_kernel, mesh_shape), grid=(token...]
where the time goes in v7:
time: 100 us
  Pallas kernels  97.8 us (98%)
  local copies, waits for them, and re-layouts  2.26 us (2%)
    pallas_call x1, Pallas kernels, finish(): pl.pallas_call(functools.partial(finish_kernel, seq_count, head_count), i...  61.7 us
    pallas_call x1, Pallas kernels, states(): pl.pallas_call(functools.partial(states_kernel, axis), grid=(owners,), in...  18.1 us
    pallas_call x1, Pallas kernels, project(): pl.pallas_call(functools.partial(project_kernel, mesh_shape), grid=(token...  18 us
    unnamed x1, local copies, waits for them, and re-layouts  2.26 us

profile of v7, /device:TPU:1, one launch (start us, length us, event | category | flops | bytes accessed | tf_op | source)
XLA Modules:
  0.0 100.1 jit_solution(17033527520175209713)
XLA Ops:
  0.0 18.0 %project.1 = (bf16[4096,512]{1,0:T(8,128)(2,1)}, f32[32,8,128]{2,1,0:T(8,128)}, bf16[32,1024]{1,0:T(8,128)(2,1)}, bf16[3,256,1024]{2,1,0:T(8,128)(2,1)}) custom-call(bf16[4096,1024]{1,0:T(8,128)(2,1)} %hidden.1, bf16[1024]{0:T(1024)(128)(2,1)} %norm_gain_ref.1, bf16[1024,256]{1,0:T(8,128)(2,1)} %vw_ref.3, bf16[1024,256]{1,0:T(8,128)(2,1)} %sw_ref.3, ...), custom_call_target="tpu_custom_call" | custom-call | tf_op jit(solution)/shard_map/project/pallas_call | solution.py:164
  18.0 18.1 %states.1 = (bf16[4,8,128,1024]{3,2,1,0:T(8,128)(2,1)}, bf16[32,2,128,256]{3,2,1,0:T(8,128)(2,1)}, f32[32,32,128]{2,1,0:T(8,128)}, f32[32,8,128]{2,1,0:T(8,128)}...) custom-call(bf16[4096,512]{1,0:T(8,128)(2,1)} %get-tuple-element.15.mix_ref.before_ref.after_ref, ...), custom_call_target="tpu_custom_call" | custom-call | tf_op jit(solution)/shard_map/states/pallas_call | solution.py:410
  36.1 61.7 %finish.1 = bf16[512,1024]{1,0:T(8,128)(2,1)} custom-call(bf16[2,128,256]{2,1,0:T(8,128)(2,1)} %get-tuple-element.18.end_ref, f32[8,256]{1,0:T(8,128)} %get-tuple-element.19.total_ref, f32[32,32,128]{2,1,0:T(8,128)} %get-tuple-element.20.cols_ref, f32[32,8,128]{2,1,0:T(8,128)} %get-tuple-element.21.row_ref, f32[4]{0:T(128)} %skip_ref.1, ...), custom_call_target="tpu_custom_call" | custom-call | tf_op jit(solution)/shard_map/finish/pallas_call | solution.py:817
  97.8 2.3 %copy.16 = bf16[512,1024]{1,0:T(8,128)(2,1)} copy(bf16[512,1024]{1,0:T(8,128)(2,1)} %finish.1) | data formatting | bytes 2097152

commit v8 on v7

--- a/solution.py
+++ b/solution.py
@@ -660,7 +660,7 @@
         wide_in[q].wait()
 
         def step(n, carry, q=q):
-            if q < 2:
+            if q == 0:
                 gates(q, n)
             for u in range(2):
                 within(q, 2 * n + u, u)
@@ -750,14 +750,6 @@
 
     ss, pieces = [], []
     for q in range(rounds):
-        if q >= 2:
-
-            def later(n, carry, q=q):
-                gates(q, n)
-                return carry
-
-            lax.fori_loop(0, owners // 2, later, 0)
-
         def some(n, sums, q=q):
             for u in range(4):
                 sums = carried(q, 4 * n + u, sums)
@@ -774,11 +766,16 @@
                 for k in range(1, head_count)
             ]
         )
-        if q:
-            pieces.append(combine(q - 1))
+        if q + 1 < rounds:
+
+            def later(n, carry, q=q):
+                gates(q + 1, n)
+                return carry
+
+            lax.fori_loop(0, owners // 2, later, 0)
+        pieces.append(combine(q))
         if q == 0:
             beside += cross()
-    pieces.append(combine(rounds - 1))
 
     for copy in late:
         copy.wait()

time: 100 us -> 109 us (1.090)
  Pallas kernels: 97.8 us -> 107 us
    pallas_call x1, Pallas kernels: 61.7 us -> 71 us  [finish(): pl.pallas_call(functools.partial(finish_kernel, seq_count, head_count), i...]
where the time goes in v8:
time: 109 us
  Pallas kernels  107 us (98%)
  local copies, waits for them, and re-layouts  2.26 us (2%)
    pallas_call x1, Pallas kernels, finish(): pl.pallas_call(functools.partial(finish_kernel, seq_count, head_count), i...  71 us
    pallas_call x1, Pallas kernels, states(): pl.pallas_call(functools.partial(states_kernel, axis), grid=(owners,), in...  18.1 us
    pallas_call x1, Pallas kernels, project(): pl.pallas_call(functools.partial(project_kernel, mesh_shape), grid=(token...  18 us
    unnamed x1, local copies, waits for them, and re-layouts  2.26 us

profile of v8, /device:TPU:1, one launch (start us, length us, event | category | flops | bytes accessed | tf_op | source)
XLA Modules:
  0.0 109.4 jit_solution(7120810553559183059)
XLA Ops:
  0.0 18.0 %project.1 = (bf16[4096,512]{1,0:T(8,128)(2,1)}, f32[32,8,128]{2,1,0:T(8,128)}, bf16[32,1024]{1,0:T(8,128)(2,1)}, bf16[3,256,1024]{2,1,0:T(8,128)(2,1)}) custom-call(bf16[4096,1024]{1,0:T(8,128)(2,1)} %hidden.1, bf16[1024]{0:T(1024)(128)(2,1)} %norm_gain_ref.1, bf16[1024,256]{1,0:T(8,128)(2,1)} %vw_ref.3, bf16[1024,256]{1,0:T(8,128)(2,1)} %sw_ref.3, ...), custom_call_target="tpu_custom_call" | custom-call | tf_op jit(solution)/shard_map/project/pallas_call | solution.py:164
  18.0 18.1 %states.1 = (bf16[4,8,128,1024]{3,2,1,0:T(8,128)(2,1)}, bf16[32,2,128,256]{3,2,1,0:T(8,128)(2,1)}, f32[32,32,128]{2,1,0:T(8,128)}, f32[32,8,128]{2,1,0:T(8,128)}...) custom-call(bf16[4096,512]{1,0:T(8,128)(2,1)} %get-tuple-element.15.mix_ref.before_ref.after_ref, ...), custom_call_target="tpu_custom_call" | custom-call | tf_op jit(solution)/shard_map/states/pallas_call | solution.py:410
  36.1 71.0 %finish.1 = bf16[512,1024]{1,0:T(8,128)(2,1)} custom-call(bf16[2,128,256]{2,1,0:T(8,128)(2,1)} %get-tuple-element.18.end_ref, f32[8,256]{1,0:T(8,128)} %get-tuple-element.19.total_ref, f32[32,32,128]{2,1,0:T(8,128)} %get-tuple-element.20.cols_ref, f32[32,8,128]{2,1,0:T(8,128)} %get-tuple-element.21.row_ref, f32[4]{0:T(128)} %skip_ref.1, ...), custom_call_target="tpu_custom_call" | custom-call | tf_op jit(solution)/shard_map/finish/pallas_call | solution.py:814
  107.1 2.3 %copy.16 = bf16[512,1024]{1,0:T(8,128)(2,1)} copy(bf16[512,1024]{1,0:T(8,128)(2,1)} %finish.1) | data formatting | bytes 2097152

commit v9 on v7

--- a/solution.py
+++ b/solution.py
@@ -556,7 +556,12 @@
         return copy
 
     travelling = []
-    for k in range(1, seq_count):
+    row = math.isqrt(seq_count)
+
+    def reach(k):
+        return sum(min(n, row - n) for n in (k % row, k // row))
+
+    for k in sorted(range(1, seq_count), key=reach, reverse=True):
         target = (me + k) % seq_count
         backward = (me + k) // seq_count
         travelling.append(

time: 100 us -> 102 us (1.020)
  Pallas kernels: 97.8 us -> 99.8 us
    pallas_call x1, Pallas kernels: 61.7 us -> 63.3 us  [finish(): pl.pallas_call(functools.partial(finish_kernel, seq_count, head_count), i...]
where the time goes in v9:
time: 102 us
  Pallas kernels  99.8 us (98%)
  local copies, waits for them, and re-layouts  2.26 us (2%)
    pallas_call x1, Pallas kernels, finish(): pl.pallas_call(functools.partial(finish_kernel, seq_count, head_count), i...  63.3 us
    pallas_call x1, Pallas kernels, states(): pl.pallas_call(functools.partial(states_kernel, axis), grid=(owners,), in...  18.5 us
    pallas_call x1, Pallas kernels, project(): pl.pallas_call(functools.partial(project_kernel, mesh_shape), grid=(token...  18 us
    unnamed x1, local copies, waits for them, and re-layouts  2.26 us

profile of v9, /device:TPU:1, one launch (start us, length us, event | category | flops | bytes accessed | tf_op | source)
XLA Modules:
  0.0 102.1 jit_solution(8456207585132953072)
XLA Ops:
  0.0 18.0 %project.1 = (bf16[4096,512]{1,0:T(8,128)(2,1)}, f32[32,8,128]{2,1,0:T(8,128)}, bf16[32,1024]{1,0:T(8,128)(2,1)}, bf16[3,256,1024]{2,1,0:T(8,128)(2,1)}) custom-call(bf16[4096,1024]{1,0:T(8,128)(2,1)} %hidden.1, bf16[1024]{0:T(1024)(128)(2,1)} %norm_gain_ref.1, bf16[1024,256]{1,0:T(8,128)(2,1)} %vw_ref.3, bf16[1024,256]{1,0:T(8,128)(2,1)} %sw_ref.3, ...), custom_call_target="tpu_custom_call" | custom-call | tf_op jit(solution)/shard_map/project/pallas_call | solution.py:164
  18.0 18.5 %states.1 = (bf16[4,8,128,1024]{3,2,1,0:T(8,128)(2,1)}, bf16[32,2,128,256]{3,2,1,0:T(8,128)(2,1)}, f32[32,32,128]{2,1,0:T(8,128)}, f32[32,8,128]{2,1,0:T(8,128)}...) custom-call(bf16[4096,512]{1,0:T(8,128)(2,1)} %get-tuple-element.15.mix_ref.before_ref.after_ref, ...), custom_call_target="tpu_custom_call" | custom-call | tf_op jit(solution)/shard_map/states/pallas_call | solution.py:410
  36.5 63.3 %finish.1 = bf16[512,1024]{1,0:T(8,128)(2,1)} custom-call(bf16[2,128,256]{2,1,0:T(8,128)(2,1)} %get-tuple-element.18.end_ref, f32[8,256]{1,0:T(8,128)} %get-tuple-element.19.total_ref, f32[32,32,128]{2,1,0:T(8,128)} %get-tuple-element.20.cols_ref, f32[32,8,128]{2,1,0:T(8,128)} %get-tuple-element.21.row_ref, f32[4]{0:T(128)} %skip_ref.1, ...), custom_call_target="tpu_custom_call" | custom-call | tf_op jit(solution)/shard_map/finish/pallas_call | solution.py:822
  99.8 2.3 %copy.16 = bf16[512,1024]{1,0:T(8,128)(2,1)} copy(bf16[512,1024]{1,0:T(8,128)(2,1)} %finish.1) | data formatting | bytes 2097152

commit v10 on v7

--- a/solution.py
+++ b/solution.py
@@ -660,7 +660,7 @@
         wide_in[q].wait()
 
         def step(n, carry, q=q):
-            if q < 2:
+            if q < 1:
                 gates(q, n)
             for u in range(2):
                 within(q, 2 * n + u, u)
@@ -750,7 +750,7 @@
 
     ss, pieces = [], []
     for q in range(rounds):
-        if q >= 2:
+        if q >= 1:
 
             def later(n, carry, q=q):
                 gates(q, n)

time: 100 us -> 100 us (level)
  no operation moved by 1% of the time
where the time goes in v10:
time: 100 us; the launch traced here: 99.7 us
  Pallas kernels  97.4 us (97%)
  local copies, waits for them, and re-layouts  2.26 us (2%)
    pallas_call x1, Pallas kernels, finish(): pl.pallas_call(functools.partial(finish_kernel, seq_count, head_count), i...  61.2 us
    pallas_call x1, Pallas kernels, states(): pl.pallas_call(functools.partial(states_kernel, axis), grid=(owners,), in...  18.1 us
    pallas_call x1, Pallas kernels, project(): pl.pallas_call(functools.partial(project_kernel, mesh_shape), grid=(token...  18 us
    unnamed x1, local copies, waits for them, and re-layouts  2.26 us

profile of v10, /device:TPU:1, one launch (start us, length us, event | category | flops | bytes accessed | tf_op | source)
XLA Modules:
  0.0 99.7 jit_solution(13995127616725180295)
XLA Ops:
  0.0 18.0 %project.1 = (bf16[4096,512]{1,0:T(8,128)(2,1)}, f32[32,8,128]{2,1,0:T(8,128)}, bf16[32,1024]{1,0:T(8,128)(2,1)}, bf16[3,256,1024]{2,1,0:T(8,128)(2,1)}) custom-call(bf16[4096,1024]{1,0:T(8,128)(2,1)} %hidden.1, bf16[1024]{0:T(1024)(128)(2,1)} %norm_gain_ref.1, bf16[1024,256]{1,0:T(8,128)(2,1)} %vw_ref.3, bf16[1024,256]{1,0:T(8,128)(2,1)} %sw_ref.3, ...), custom_call_target="tpu_custom_call" | custom-call | tf_op jit(solution)/shard_map/project/pallas_call | solution.py:164
  18.0 18.1 %states.1 = (bf16[4,8,128,1024]{3,2,1,0:T(8,128)(2,1)}, bf16[32,2,128,256]{3,2,1,0:T(8,128)(2,1)}, f32[32,32,128]{2,1,0:T(8,128)}, f32[32,8,128]{2,1,0:T(8,128)}...) custom-call(bf16[4096,512]{1,0:T(8,128)(2,1)} %get-tuple-element.15.mix_ref.before_ref.after_ref, ...), custom_call_target="tpu_custom_call" | custom-call | tf_op jit(solution)/shard_map/states/pallas_call | solution.py:410
  36.1 61.2 %finish.1 = bf16[512,1024]{1,0:T(8,128)(2,1)} custom-call(bf16[2,128,256]{2,1,0:T(8,128)(2,1)} %get-tuple-element.18.end_ref, f32[8,256]{1,0:T(8,128)} %get-tuple-element.19.total_ref, f32[32,32,128]{2,1,0:T(8,128)} %get-tuple-element.20.cols_ref, f32[32,8,128]{2,1,0:T(8,128)} %get-tuple-element.21.row_ref, f32[4]{0:T(128)} %skip_ref.1, ...), custom_call_target="tpu_custom_call" | custom-call | tf_op jit(solution)/shard_map/finish/pallas_call | solution.py:817
  97.4 2.3 %copy.16 = bf16[512,1024]{1,0:T(8,128)(2,1)} copy(bf16[512,1024]{1,0:T(8,128)(2,1)} %finish.1) | data formatting | bytes 2097152
